TPU v7x, 32 devices: a whole 2x2x4 slice. The times are simulated.
32 devices in a mesh: group: 2 (over x), blk: 16 (over z, y, core).
Axes of the slice: x: 2, y: 2, z: 4, core: 2. Of those that a mesh axis runs over, the one named last changes fastest.
Arguments:
- queries: bfloat16 [4, 64, 2048], P('group', 'blk'), parts along dimension 0, may hold values from -160 to 160
- keys: bfloat16 [4, 20480, 256], P('group', 'blk'), parts along dimension 0, may hold values from -4 to 4
- values: bfloat16 [4, 20480, 256], P('group', 'blk'), parts along dimension 0, may hold values from -6 to 6
- lengths: int32 [4], P('group'), parts along dimension 0, may hold values from 15360 to 20480
- offsets: int32 [4], P('group'), parts along dimension 0, may hold values from 12800 to 20416
Outputs:
- attended: bfloat16 [4, 64, 2048], P('group', 'blk'), parts along dimension 0
There are 2 independent parts, one for each index of `group`. A program takes and returns all parts, laid end to end along the dimension named above; each array names one. Nothing has to cross between parts.
All inputs are finite; a program needn't handle non-finite values.
Results may differ from a plain program's by a relative error of at most 0.0085.
Values may be sent and summed in bfloat16 or wider, within the bound.
No kernel may reach another device: no remote copies, remote signals or barrier semaphores. Data moves between devices by JAX's collectives and lax.ppermute only.
A program may use at most 64 MiB of HBM per device.

v0:
```python
import math

import jax
import jax.numpy as jnp
from jax import lax
from jax.sharding import PartitionSpec as P

KV_HEADS = 2
HEAD_DIM = 128


masked_low = -1e30


def shard_partial(query_rows, key_rows, value_rows, query_pos, key_pos, lengths):
    micro_count, rows_count, row_width = query_rows.shape
    heads_count = row_width // HEAD_DIM
    group_size = heads_count // KV_HEADS
    query_split = query_rows.reshape(micro_count, rows_count, KV_HEADS, group_size, HEAD_DIM)
    key_split = key_rows.reshape(micro_count, key_rows.shape[1], KV_HEADS, HEAD_DIM)
    value_split = value_rows.reshape(micro_count, value_rows.shape[1], KV_HEADS, HEAD_DIM)
    scores = jnp.einsum(
        "brkgd,bskd->bkgrs", query_split, key_split, preferred_element_type=jnp.float32
    )
    scores = scores * (1.0 / math.sqrt(HEAD_DIM))
    visible = (key_pos[None, None, :] <= query_pos[:, :, None]) & (
        key_pos[None, None, :] < lengths[:, None, None]
    )
    visible = visible[:, None, None, :, :]
    any_visible = jnp.any(visible, axis=-1)
    row_max = jnp.max(jnp.where(visible, scores, masked_low), axis=-1)
    safe_max = jnp.where(any_visible, row_max, 0.0)
    shifted = jnp.where(visible, scores - safe_max[..., None], 0.0)
    weights = jnp.where(visible, jnp.exp(shifted), 0.0)
    totals = jnp.sum(weights, axis=-1)
    bounded = jnp.maximum(totals, 1.0)
    numerator = jnp.einsum(
        "bkgrs,bskd->bkgrd",
        weights.astype(jnp.bfloat16),
        value_split,
        preferred_element_type=jnp.float32,
    )
    partial_value = (numerator / bounded[..., None]).astype(jnp.bfloat16)
    partial_value = jnp.transpose(partial_value, (0, 3, 1, 2, 4)).reshape(
        micro_count, rows_count, row_width
    )
    logsum = jnp.where(any_visible, safe_max + jnp.log(bounded), masked_low)
    logsum = jnp.transpose(logsum, (0, 3, 1, 2)).reshape(micro_count, rows_count, heads_count)
    return (partial_value, logsum)


def body(queries, keys, values, lengths, offsets):
    micro_count, local_rows, row_width = queries.shape
    local_keys = keys.shape[1]
    heads_count = row_width // HEAD_DIM
    shards = lax.axis_size("blk")
    key_pos = lax.axis_index("blk") * local_keys + jnp.arange(local_keys, dtype=jnp.int32)
    visiting = lax.all_gather(queries, "blk", axis=1, tiled=True)
    rows_count = visiting.shape[1]
    block_rows = math.gcd(rows_count, 64)
    block_count = rows_count // block_rows

    def one_block(block_index):
        block_start = block_index * block_rows
        selected = lax.dynamic_slice_in_dim(visiting, block_start, block_rows, 1)
        query_pos = (
            offsets[:, None] + block_start + jnp.arange(block_rows, dtype=jnp.int32)[None, :]
        )
        return shard_partial(selected, keys, values, query_pos, key_pos, lengths)

    block_parts, block_logs = lax.map(one_block, jnp.arange(block_count, dtype=jnp.int32))
    block_parts = jnp.moveaxis(block_parts, 0, 1).reshape(micro_count, rows_count, row_width)
    block_logs = jnp.moveaxis(block_logs, 0, 1).reshape(micro_count, rows_count, heads_count)
    partials = block_parts
    logsums = block_logs
    partials, logsums = (partials, logsums)
    shaped_parts = partials.reshape(micro_count, shards, local_rows, row_width)
    shaped_logs = logsums.reshape(micro_count, shards, local_rows, heads_count)
    home_parts = lax.all_to_all(shaped_parts, "blk", split_axis=1, concat_axis=1, tiled=True)
    home_logs = lax.all_to_all(shaped_logs, "blk", split_axis=1, concat_axis=1, tiled=True)
    row_peak = jnp.max(home_logs, axis=1, keepdims=True)
    scales = jnp.exp(home_logs - row_peak)
    denominator = jnp.sum(scales, axis=1)
    split_parts = home_parts.reshape(micro_count, shards, local_rows, heads_count, HEAD_DIM)
    weighted = jnp.sum(split_parts * scales[..., None], axis=1)
    merged = weighted / denominator[..., None]
    attended = merged.reshape(micro_count, local_rows, row_width).astype(jnp.bfloat16)
    return attended


def solution(mesh):
    return jax.shard_map(
        body,
        mesh=mesh,
        in_specs=(
            P("group", "blk", None),
            P("group", "blk", None),
            P("group", "blk", None),
            P("group"),
            P("group"),
        ),
        out_specs=P("group", "blk", None),
        check_vma=False,
    )
```

profile of v0, /device:TPU:0, one launch (start us, length us, event | category | flops | bytes accessed | tf_op | source)
XLA Modules:
  0.0 72.9 jit_solution(13449058837468919631)
XLA Ops:
  0.0 0.7 iota_add_fusion.1
  0.7 0.7 %broadcast_compare_fusion = pred[2,1280]{1,0:T(4,128)(4,1)S(1)} fusion(s32[1280]{0:T(1024)S(1)} %iota_add_fusion, s32[2]{0:T(128)} %param.8), kind=kLoop, calls=%fused_computation.26 | loop fusion | flops 2560 | bytes 7688 | tf_op jit(solution)/shard_map/while/body/eval_jaxpr/lt | solution.py:27
  1.5 0.2 compare_and_fusion
  1.6 0.3 and_reduce_fusion
  1.9 3.0 %reshape.92 = bf16[2,1280,2,128]{3,2,1,0:T(2,128)(2,1)S(1)} reshape(bf16[2,1280,256]{2,1,0:T(8,128)(2,1)} %param.6) | data formatting | bytes 2621440 | tf_op jit(solution)/shard_map/while/body/eval_jaxpr/reshape | solution.py:20
  4.9 0.8 %copy.24 = bf16[2,4,2048]{2,0,1:T(2,128)(2,1)S(1)} copy(bf16[2,4,2048]{2,1,0:T(4,128)(2,1)} %param.5) | data formatting | bytes 65536 | tf_op args[0]
  5.7 24.6 %all_gather.3 = bf16[2,64,2048]{2,0,1:T(2,128)(2,1)S(1)} all-gather(bf16[2,4,2048]{2,0,1:T(2,128)(2,1)S(1)} %copy.24), channel_id=1, replica_groups=mesh['group'=2,'blk'=16] {'blk'}, dimensions={1}, use_global_device_ids=true | all-gather | bytes 557056 | tf_op jit(solution)/shard_map/all_gather | solution.py:58
  30.3 0.3 reshape.97
  30.6 0.0 copy-start.1
  30.6 2.2 %fusion = (f32[2,2,8,64]{3,2,1,0:T(8,128)S(1)}, f32[2,2,1280,64,8]{2,3,4,1,0:T(8,128)S(1)}) fusion(pred[2,64,1280]{2,1,0:T(8,128)(4,1)S(1)} %compare_and_fusion, bf16[2,64,2,8,128]{4,3,2,0,1:T(8,128)(2,1)S(1)} %reshape.97, bf16[2,1280,2,128,1]{3,2,1,0,4:T(2,128)(2,1)S(1)} %bitcast.50), kind=kOutput, calls=%fused_computation.2 | convolution fusion | flops 678950912 | bytes 12492800 | tf_op jit(solution)/shard_map/while/body/eval_jaxpr/brkgd,bskd->bkgrs/dot_general | solution.py:22
  32.8 0.0 copy-start
  32.8 4.0 %copy-done = f32[2,2,1280,64,8]{2,3,4,1,0:T(8,128)} copy-done((f32[2,2,1280,64,8]{2,3,4,1,0:T(8,128)}, f32[2,2,1280,64,8]{2,3,4,1,0:T(8,128)S(1)}, u32[]{:S(2)}) %copy-start) | copy-done | bytes 10485784
  36.8 3.2 %fusion.4 = f32[2,2,8,64]{3,2,1,0:T(8,128)S(1)} fusion(f32[2,2,1280,64,8]{2,3,4,1,0:T(8,128)S(1)} %get-tuple-element.24, f32[2,2,8,64]{3,2,1,0:T(8,128)S(1)} %broadcast_select_fusion, pred[2,64,1280]{2,1,0:T(8,128)(4,1)S(1)} %compare_and_fusion), kind=kLoop, calls=%fused_computation.6 | loop fusion | flops 13105152 | bytes 10665984 | tf_op jit(solution)/shard_map/while/body/eval_jaxpr/reduce_sum | solution.py:35
  40.0 0.1 copy.31
  40.1 0.1 reshape_reshape_transpose.7
  40.2 0.7 reshape.98
  40.9 3.5 %all-to-all-start.1 = ((f32[16,1,128]{2,1,0:T(1,128)}), f32[16,1,128]{2,1,0:T(1,128)S(1)}, u32[]{:S(2)}, u32[]{:S(2)}) async-start(f32[16,1,128]{2,1,0:T(1,128)} %reshape.98), calls=%async_computation.1 | async-start | bytes 16384 | tf_op jit(solution)/shard_map/all_to_all | solution.py:80
  44.4 0.0 copy-done.1
  44.4 0.3 reshape.94
  44.8 5.4 %divide_convert_fusion = bf16[2,64,2,8,128]{4,1,3,2,0:T(8,128)(2,1)S(1)} fusion(bf16[2,1280,2,128,1]{3,2,1,0,4:T(2,128)(2,1)S(1)} %bitcast.51, f32[2,2,1280,64,8]{2,3,4,1,0:T(8,128)} %copy-done, f32[2,2,8,64]{3,2,1,0:T(8,128)S(1)} %broadcast_select_fusion, pred[2,64,1280]{2,1,0:T(8,128)(4,1)S(1)} %compare_and_fusion, ...), kind=kOutput, calls=%fused_computation.15 | convolution fusion | flops 684720128 | bytes 12500992 | tf_op jit(solution)/shard_map/while/body/eval_jaxpr/bkgrs,bskd->bkgrd/dot_general | solution.py:37
  50.2 0.3 copy.29
  50.5 0.1 reshape_reshape_transpose.6
  50.7 1.0 %copy.30 = bf16[2,16,4,2048]{3,2,0,1:T(4,128)(2,1)} copy(bf16[2,16,4,2048]{3,2,1,0:T(4,128)(2,1)S(1)} %reshape_reshape_transpose.6) | data formatting | bytes 1048576 | tf_op jit(solution)/shard_map/reshape;reshape;transpose | solution.py:77
  51.7 0.0 all-to-all-done.1
  51.7 6.0 %all-to-all-start = ((bf16[2,16,4,2048]{3,2,0,1:T(4,128)(2,1)}), bf16[2,16,4,2048]{3,2,0,1:T(4,128)(2,1)S(1)}, u32[]{:S(2)}, u32[]{:S(2)}) async-start(bf16[2,16,4,2048]{3,2,0,1:T(4,128)(2,1)} %copy.30), calls=%async_computation | async-start | bytes 1048576 | tf_op jit(solution)/shard_map/all_to_all | solution.py:79
  57.7 0.5 broadcast.111
  58.2 0.7 reduce.2
  58.9 0.1 reshape.99
  59.0 0.3 mul.26
  59.4 0.4 mul.27
  59.7 0.1 div.26
  59.9 12.1 %all-to-all-done = bf16[2,16,4,2048]{3,2,0,1:T(4,128)(2,1)S(1)} async-done(((bf16[2,16,4,2048]{3,2,0,1:T(4,128)(2,1)}), bf16[2,16,4,2048]{3,2,0,1:T(4,128)(2,1)S(1)}, u32[]{:S(2)}, u32[]{:S(2)}) %all-to-all-start) | async-done | bytes 524320 | tf_op jit(solution)/shard_map/all_to_all | solution.py:79
  72.0 0.3 multiply_reduce_fusion
  72.3 0.6 divide_convert_fusion.1
  (8 shorter events, 0.1 us)
Async XLA Ops:
  30.6 13.8 %copy-start.1 = (bf16[2,1280,256]{2,1,0:T(8,128)(2,1)S(1)}, bf16[2,1280,256]{2,1,0:T(8,128)(2,1)}, u32[]{:S(2)}) copy-start(bf16[2,1280,256]{2,1,0:T(8,128)(2,1)} %param.7) | copy-start | bytes 3932164
  32.8 4.0 %copy-start = (f32[2,2,1280,64,8]{2,3,4,1,0:T(8,128)}, f32[2,2,1280,64,8]{2,3,4,1,0:T(8,128)S(1)}, u32[]{:S(2)}) copy-start(f32[2,2,1280,64,8]{2,3,4,1,0:T(8,128)S(1)} %get-tuple-element.24) | copy-start | bytes 31457284
  40.9 10.8 %all-to-all-start.1 = ((f32[16,1,128]{2,1,0:T(1,128)}), f32[16,1,128]{2,1,0:T(1,128)S(1)}, u32[]{:S(2)}, u32[]{:S(2)}) async-start(f32[16,1,128]{2,1,0:T(1,128)} %reshape.98), calls=%async_computation.1 | async-start | bytes 16384 | tf_op jit(solution)/shard_map/all_to_all | solution.py:80
  51.7 20.2 %all-to-all-start = ((bf16[2,16,4,2048]{3,2,0,1:T(4,128)(2,1)}), bf16[2,16,4,2048]{3,2,0,1:T(4,128)(2,1)S(1)}, u32[]{:S(2)}, u32[]{:S(2)}) async-start(bf16[2,16,4,2048]{3,2,0,1:T(4,128)(2,1)} %copy.30), calls=%async_computation | async-start | bytes 1048576 | tf_op jit(solution)/shard_map/all_to_all | solution.py:79
where the time goes:
time: 73.3 us; the launch traced here: 72.9 us
  blocking collectives  24.6 us (34%)
  local copies, waits for them, and re-layouts  12.3 us (17%)
  waiting for transfers between devices  12.1 us (17%)
  starting transfers between devices  9.44 us (13%)
  matrix products  7.53 us (10%)
  other arithmetic  6.77 us (9%)
    all_gather x1, blocking collectives, body(): visiting = lax.all_gather(queries, 'blk', axis=1, tiled=True)  24.6 us
    all_to_all x1, waiting for transfers between devices, body(): lax.all_to_all(shaped_parts, 'blk', split_axis=1, concat_axis=1, tiled=True)  12.1 us
    all_to_all x1, starting transfers between devices, body(): lax.all_to_all(shaped_parts, 'blk', split_axis=1, concat_axis=1, tiled=True)  5.97 us
    unnamed x7, local copies, waits for them, and re-layouts  5.58 us
    dot_general x1, matrix products, shard_partial(): jnp.einsum('bkgrs,bskd->bkgrd', weights.astype(jnp.bfloat16), value_split...  5.37 us
    all_to_all x1, starting transfers between devices, body(): lax.all_to_all(shaped_logs, 'blk', split_axis=1, concat_axis=1, tiled=True)  3.47 us
    reduce_sum x1, other arithmetic, shard_partial(): totals = jnp.sum(weights, axis=-1)  3.17 us
    reshape x1, local copies, waits for them, and re-layouts, shard_partial(): key_rows.reshape(micro_count, key_rows.shape[1], KV_HEADS, HEAD_DIM)  2.96 us
  transfers between devices with their start and end apart: 2, of which 1 were waited for; matrix products, arithmetic and copies ran while one was open for 13% of the time, Pallas kernels for 0%

commit v1 on v0

v1 whole, which is shorter than its diff:
```python
import functools
import math

import jax
import jax.numpy as jnp
from jax import lax
from jax.experimental import pallas as pl
from jax.experimental.pallas import tpu as pltpu
from jax.sharding import PartitionSpec as P

KV_HEADS = 2
HEAD_DIM = 128
LOW = -1e30
STAT_ROWS = 8

VMEM = pl.BlockSpec(memory_space=pltpu.VMEM)
SMEM = pl.BlockSpec(memory_space=pltpu.SMEM)


def digit_masks(shards):
    assert shards >= 16 and shards & (shards - 1) == 0 and shards.bit_length() % 2 == 1
    masks = [[1], [2]]
    unit = 4
    wide = []
    while unit < shards:
        wide.append([unit, 2 * unit, 3 * unit])
        unit *= 4
    return masks + wide[::-1]


def pairs(shards, mask):
    return [(i, i ^ mask) for i in range(shards)]


def split3(x):
    high = x.astype(jnp.bfloat16)
    rest = x - high.astype(jnp.float32)
    mid = rest.astype(jnp.bfloat16)
    low = (rest - mid.astype(jnp.float32)).astype(jnp.bfloat16)
    return [part.astype(jnp.float32) for part in (high, mid, low)]


def packed(num, peak, total):
    rows = split3(peak) + split3(total)
    rows.append(jnp.zeros((STAT_ROWS - len(rows), num.shape[1]), jnp.float32))
    return jnp.concatenate([num] + rows, axis=0).astype(jnp.bfloat16)


def unpacked(block):
    block = block.astype(jnp.float32)
    stats = block[HEAD_DIM:]
    peak = (stats[0:1] + stats[1:2]) + stats[2:3]
    total = (stats[3:4] + stats[4:5]) + stats[5:6]
    return block[:HEAD_DIM], peak, total


def kept(num, peak, total):
    pad = jnp.zeros((STAT_ROWS - 2, num.shape[1]), jnp.float32)
    return jnp.concatenate([num, peak, total, pad], axis=0)


def unkept(block):
    return block[:HEAD_DIM], block[HEAD_DIM : HEAD_DIM + 1], block[HEAD_DIM + 1 : HEAD_DIM + 2]


def merged(parts):
    peak = functools.reduce(jnp.maximum, [part[1] for part in parts])
    scales = [jnp.exp2(part[1] - peak) for part in parts]
    num = sum(part[0] * scale for part, scale in zip(parts, scales))
    total = sum(part[2] * scale for part, scale in zip(parts, scales))
    return num, peak, total


def transpose_kernel(v_ref, vt_ref):
    for micro in range(v_ref.shape[0]):
        vt_ref[micro] = v_ref[micro].T


def attend_kernel(local_rows, lane_masks, send, info_ref, len_ref, off_ref, q_ref, k_ref, vt_ref, out_ref):
    groups, lanes, _ = q_ref.shape
    key_count = k_ref.shape[1]
    me = info_ref[0]
    width = lanes // len(lane_masks)
    lane = lax.broadcasted_iota(jnp.int32, (1, lanes), 1)
    origin = jnp.full((1, lanes), lane_masks[0], jnp.int32)
    for index, mask in enumerate(lane_masks):
        origin = jnp.where(lane // width == index, mask, origin)
    row = (origin ^ me) * local_rows + lane % local_rows
    unit = math.log2(math.e) / math.sqrt(HEAD_DIM)
    key = lax.broadcasted_iota(jnp.int32, (key_count, lanes), 0)
    for group in range(groups):
        micro, head = divmod(group, KV_HEADS)
        last = jnp.minimum(off_ref[micro] + row, len_ref[micro] - 1) - me * key_count
        span = slice(head * HEAD_DIM, (head + 1) * HEAD_DIM)
        scores = lax.dot_general(
            k_ref[micro, :, span],
            q_ref[group],
            (((1,), (1,)), ((), ())),
            preferred_element_type=jnp.float32,
        )
        scores = jnp.where(key <= last, scores, LOW)
        top = jnp.max(scores, axis=0, keepdims=True)
        some = last >= 0
        top = jnp.where(some, top, 0.0)
        weights = jnp.exp2((scores - top) * unit)
        total = jnp.sum(weights, axis=0, keepdims=True)
        num = jnp.dot(
            vt_ref[micro, span, :], weights.astype(jnp.bfloat16), preferred_element_type=jnp.float32
        )
        peak = jnp.where(some, top * unit, LOW)
        out_ref[group] = packed(num, peak, total) if send else kept(num, peak, total)


def merge_kernel(ways, received, keep_ref, *refs):
    got_refs, own_ref, send_refs = refs[:received], refs[received], refs[received + 1 :]
    groups, _, lanes = keep_ref.shape
    width = lanes // ways
    for group in range(groups):
        parts = [unkept(keep_ref[group])] + [unpacked(got[group]) for got in got_refs]
        num, peak, total = merged(parts)
        for way in range(ways):
            span = slice(way * width, (way + 1) * width)
            part = (num[:, span], peak[:, span], total[:, span])
            if way == 0:
                own_ref[group] = kept(*part)
            else:
                send_refs[way - 1][group] = packed(*part)


def gather_lanes(blocks, way, width):
    lanes = blocks[0].shape[1]
    lane = lax.broadcasted_iota(jnp.int32, (1, lanes), 1) // width
    picked = None
    for group, block in enumerate(blocks):
        shift = (group - way) * width % lanes
        moved = pltpu.roll(block, shift, 1) if shift else block
        picked = moved if picked is None else jnp.where(lane == group, moved, picked)
    return picked


def merge_repack_kernel(ways, received, keep_ref, *refs):
    got_refs, own_ref, send_refs = refs[:received], refs[received], refs[received + 1 :]
    groups, _, lanes = keep_ref.shape
    width = lanes // ways
    done = []
    for group in range(groups):
        parts = [unkept(keep_ref[group])] + [unpacked(got[group]) for got in got_refs]
        done.append(kept(*merged(parts)))
    for way in range(ways):
        block = gather_lanes(done, way, width)
        if way == 0:
            own_ref[...] = block
        else:
            send_refs[way - 1][...] = packed(*unkept(block))


def final_kernel(keep_ref, *refs):
    got_refs, out_ref = refs[:-1], refs[-1]
    parts = [unkept(keep_ref[...])] + [unpacked(got[...]) for got in got_refs]
    num, _, total = merged(parts)
    out_ref[...] = (num / total).T.astype(jnp.bfloat16)


def call(kernel, outs, specs, flops=0, nbytes=0, grant=4):
    return pl.pallas_call(
        kernel,
        out_shape=outs,
        in_specs=specs,
        out_specs=jax.tree.map(lambda _: VMEM, outs),
        cost_estimate=pl.CostEstimate(flops=flops, bytes_accessed=nbytes, transcendentals=0),
        compiler_params=pltpu.CompilerParams(vmem_limit_bytes=grant << 20),
    )


def struct(shape, dtype):
    return jax.ShapeDtypeStruct(shape, dtype)


def body(queries, keys, values, lengths, offsets):
    micro_count, local_rows, row_width = queries.shape
    heads = row_width // HEAD_DIM
    share = heads // KV_HEADS
    groups = micro_count * KV_HEADS
    width = share * local_rows
    shards = lax.axis_size("blk")
    masks = digit_masks(shards)
    stacked = HEAD_DIM + STAT_ROWS
    info = jnp.reshape(lax.axis_index("blk"), (1,)).astype(jnp.int32)

    own = queries.reshape(micro_count, local_rows, KV_HEADS, share, HEAD_DIM)
    own = own.transpose(0, 2, 3, 1, 4).reshape(groups, width, HEAD_DIM)
    values_t = call(
        transpose_kernel, struct((micro_count, values.shape[2], values.shape[1]), values.dtype), [VMEM]
    )(values)

    origin = [0]
    piece = own
    for level in masks[:1:-1]:
        piece = jnp.concatenate(
            [piece] + [lax.ppermute(piece, "blk", pairs(shards, mask)) for mask in level], axis=1
        )
        origin = [base ^ mask for mask in [0] + level for base in origin]
    near = piece
    far = lax.ppermute(near, "blk", pairs(shards, 2))
    near_far = jnp.concatenate([near, far], axis=1)
    across = lax.ppermute(near_far, "blk", pairs(shards, 1))
    near_origin = origin + [base ^ 2 for base in origin]

    lanes = near_far.shape[1]

    def attend(rows, mask, send):
        return call(
            functools.partial(attend_kernel, local_rows, [base ^ mask for base in near_origin], send),
            struct((groups, stacked, lanes), jnp.bfloat16 if send else jnp.float32),
            [SMEM, SMEM, SMEM, VMEM, VMEM, VMEM],
            flops=4 * groups * lanes * keys.shape[1] * HEAD_DIM,
            grant=24,
        )(info, lengths, offsets, rows, keys, values_t)

    sends = attend(across, 1, True)
    got = [lax.ppermute(sends, "blk", pairs(shards, 1))]
    keep = attend(near_far, 0, False)
    for step in range(1, len(masks)):
        level = masks[step]
        ways = len(level) + 1
        if step < len(masks) - 1:
            kernel = merge_kernel
            shape = (groups, stacked, lanes // ways)
        else:
            kernel = merge_repack_kernel
            shape = (stacked, groups * width)
        lanes //= ways
        outs = [struct(shape, jnp.float32)] + [struct(shape, jnp.bfloat16)] * len(level)
        keep, *sends = call(
            functools.partial(kernel, ways, len(got)), outs, [VMEM] * (1 + len(got))
        )(keep, *got)
        got = [lax.ppermute(part, "blk", pairs(shards, mask)) for part, mask in zip(sends, level)]
    merged_rows = call(
        final_kernel, struct((groups * width, HEAD_DIM), jnp.bfloat16), [VMEM] * (1 + len(got))
    )(keep, *got)
    shaped = merged_rows.reshape(micro_count, KV_HEADS, share, local_rows, HEAD_DIM)
    return shaped.transpose(0, 3, 1, 2, 4).reshape(micro_count, local_rows, row_width)


def solution(mesh):
    return jax.shard_map(
        body,
        mesh=mesh,
        in_specs=(
            P("group", "blk", None),
            P("group", "blk", None),
            P("group", "blk", None),
            P("group"),
            P("group"),
        ),
        out_specs=P("group", "blk", None),
        check_vma=False,
    )
```

time: 73.3 us -> 42.4 us (0.58)
  blocking collectives: 24.6 us -> 0 us
  Pallas kernels: 0 us -> 9.71 us
  local copies, waits for them, and re-layouts: 12.3 us -> 3.07 us
  matrix products: 7.53 us -> 0 us
  other arithmetic: 6.77 us -> 0.77 us
  starting transfers between devices: 9.44 us -> 13.9 us
  waiting for transfers between devices: 12.1 us -> 14.6 us
    all_gather x1 -> x0, blocking collectives: 24.6 us -> none  [body(): visiting = lax.all_gather(queries, 'blk', axis=1, tiled=True)]
    ppermute x0 -> x10, waiting for transfers between devices: none -> 14.6 us  [the longest x4 7.52 us: body(): lax.ppermute(part, 'blk', pairs(shards, mask))]
    ppermute x0 -> x10, starting transfers between devices: none -> 13.9 us  [the longest x4 6.03 us: body(): lax.ppermute(part, 'blk', pairs(shards, mask))]
    all_to_all x2 -> x0, waiting for transfers between devices: 12.1 us -> none  [the longest x1 12.1 us: body(): lax.all_to_all(shaped_parts, 'blk', split_axis=1, concat_axis=1, tiled=True)]
    pallas_call x0 -> x6, Pallas kernels: none -> 9.71 us  [the longest x2 8.22 us: attend(): call(functools.partial(attend_kernel, local_rows, [base ^ mask for base i...]
    all_to_all x2 -> x0, starting transfers between devices: 9.44 us -> none  [the longest x1 5.97 us: body(): lax.all_to_all(shaped_parts, 'blk', split_axis=1, concat_axis=1, tiled=True)]
    dot_general x2 -> x0, matrix products: 7.53 us -> none  [the longest x1 5.37 us: shard_partial(): jnp.einsum('bkgrs,bskd->bkgrd', weights.astype(jnp.bfloat16), value_split...]
    reshape x3 -> x0, local copies, waits for them, and re-layouts: 3.64 us -> none  [the longest x1 2.96 us: shard_partial(): key_rows.reshape(micro_count, key_rows.shape[1], KV_HEADS, HEAD_DIM)]
  transfers between devices with their start and end apart: 2 -> 10, of which waited for: 1 -> 6; matrix products, arithmetic and copies ran while one was open for 13% -> 2% of each run, Pallas kernels for 0% -> 11%
where the time goes in v1:
time: 42.4 us; the launch traced here: 42.1 us
  waiting for transfers between devices  14.6 us (34%)
  starting transfers between devices  13.9 us (33%)
  Pallas kernels  9.71 us (23%)
  local copies, waits for them, and re-layouts  3.07 us (7%)
  other arithmetic  0.77 us (2%)
    pallas_call x2, Pallas kernels, attend(): call(functools.partial(attend_kernel, local_rows, [base ^ mask for base i...  8.22 us
    ppermute x4, waiting for transfers between devices, body(): lax.ppermute(part, 'blk', pairs(shards, mask))  7.52 us
    ppermute x4, starting transfers between devices, body(): lax.ppermute(part, 'blk', pairs(shards, mask))  6.03 us
    ppermute x3, starting transfers between devices, body(): lax.ppermute(piece, 'blk', pairs(shards, mask))  5.64 us
    ppermute x3, waiting for transfers between devices, body(): lax.ppermute(piece, 'blk', pairs(shards, mask))  3.66 us
    ppermute x1, waiting for transfers between devices, body(): far = lax.ppermute(near, 'blk', pairs(shards, 2))  3.42 us
    unnamed x12, local copies, waits for them, and re-layouts  3.05 us
    ppermute x1, starting transfers between devices, body(): far = lax.ppermute(near, 'blk', pairs(shards, 2))  1.58 us
  transfers between devices with their start and end apart: 10, of which 6 were waited for; matrix products, arithmetic and copies ran while one was open for 2% of the time, Pallas kernels for 11%

profile of v1, /device:TPU:0, one launch (start us, length us, event | category | flops | bytes accessed | tf_op | source)
XLA Modules:
  0.0 42.1 jit_solution(1445441466387791680)
XLA Ops:
  0.0 5.1 %collective-permute-start.2 = (bf16[4,32,128]{2,1,0:T(8,128)(2,1)}, bf16[4,32,128]{2,1,0:T(8,128)(2,1)S(1)}, u32[]{:S(2)}, u32[]{:S(2)}) collective-permute-start(bf16[4,32,128]{2,1,0:T(8,128)(2,1)} %bitcast.11), channel_id=1, source_target_pairs={{0,12},{1,13},{2,14},{3,15},{4,8},{5,9},{6,10},{7,11},{8,4},{9,5},... | collective-permute-start | bytes 98312 | tf_op jit(solution)/shard_map/ppermute | solution.py:200
  5.1 0.0 collective-permute-start.1
  5.1 0.6 %collective-permute-start = (bf16[4,32,128]{2,1,0:T(8,128)(2,1)}, bf16[4,32,128]{2,1,0:T(8,128)(2,1)S(1)}, u32[]{:S(2)}, u32[]{:S(2)}) collective-permute-start(bf16[4,32,128]{2,1,0:T(8,128)(2,1)} %bitcast.13), channel_id=1, source_target_pairs={{0,4},{1,5},{2,6},{3,7},{4,0},{5,1},{6,2},{7,3},{8,12},{9,13},{10,... | collective-permute-start | bytes 98312 | tf_op jit(solution)/shard_map/ppermute | solution.py:200
  5.6 0.8 %constant_dynamic-update-slice_fusion.4 = bf16[4,256,128]{2,1,0:T(8,128)(2,1)S(1)} fusion(bf16[4,32,128]{2,1,0:T(8,128)(2,1)} %bitcast.14), kind=kLoop, calls=%fused_computation.5 | loop fusion | bytes 65536
  6.4 0.7 %collective-permute-done.2 = bf16[4,32,128]{2,1,0:T(8,128)(2,1)S(1)} collective-permute-done((bf16[4,32,128]{2,1,0:T(8,128)(2,1)}, bf16[4,32,128]{2,1,0:T(8,128)(2,1)S(1)}, u32[]{:S(2)}, u32[]{:S(2)}) %collective-permute-start.2) | collective-permute-done | bytes 32800 | tf_op jit(solution)/shard_map/ppermute | solution.py:200
  7.2 2.9 %collective-permute-done.1 = bf16[4,32,128]{2,1,0:T(8,128)(2,1)S(1)} collective-permute-done((bf16[4,32,128]{2,1,0:T(8,128)(2,1)}, bf16[4,32,128]{2,1,0:T(8,128)(2,1)S(1)}, u32[]{:S(2)}, u32[]{:S(2)}) %collective-permute-start.1) | collective-permute-done | bytes 32800 | tf_op jit(solution)/shard_map/ppermute | solution.py:200
  10.1 0.0 collective-permute-done
  10.1 0.8 %pad_maximum_fusion = bf16[4,128,128]{2,1,0:T(8,128)(2,1)S(1)} fusion(bf16[4,32,128]{2,1,0:T(8,128)(2,1)S(1)} %collective-permute-done.2, bf16[4,32,128]{2,1,0:T(8,128)(2,1)S(1)} %collective-permute-done.1, bf16[4,32,128]{2,1,0:T(8,128)(2,1)S(1)} %collective-permute-done, bf16[4,32,128]{2,1,0:T(8,128)(2,1)} %bitcast.15), kind=kLoop, calls=%fused_computation | loop fusion | flops 524288 | bytes 262144 | tf_op jit(solution)/shard_map/concatenate | solution.py:199
  10.9 1.6 %collective-permute-start.3 = (bf16[4,128,128]{2,1,0:T(8,128)(2,1)S(1)}, bf16[4,128,128]{2,1,0:T(8,128)(2,1)S(1)}, u32[]{:S(2)}, u32[]{:S(2)}) collective-permute-start(bf16[4,128,128]{2,1,0:T(8,128)(2,1)S(1)} %pad_maximum_fusion), channel_id=1, source_target_pairs={{0,2},{1,3},{2,0},{3,1},{4,6},{5,7},{6,4},{7,5},{8,10},{9,11},{10,... | collective-permute-start | bytes 393224 | tf_op jit(solution)/shard_map/ppermute | solution.py:204
  12.5 3.4 %collective-permute-done.3 = bf16[4,128,128]{2,1,0:T(8,128)(2,1)S(1)} collective-permute-done((bf16[4,128,128]{2,1,0:T(8,128)(2,1)S(1)}, bf16[4,128,128]{2,1,0:T(8,128)(2,1)S(1)}, u32[]{:S(2)}, u32[]{:S(2)}) %collective-permute-start.3) | collective-permute-done | bytes 131104 | tf_op jit(solution)/shard_map/ppermute | solution.py:204
  15.9 0.1 collective-permute-start.4
  16.0 0.0 copy-start.1
  16.0 1.3 %copy-done.1 = bf16[2,1280,256]{2,1,0:T(8,128)(2,1)S(1)} copy-done((bf16[2,1280,256]{2,1,0:T(8,128)(2,1)S(1)}, bf16[2,1280,256]{2,1,0:T(8,128)(2,1)}, u32[]{:S(2)}) %copy-start.1) | copy-done | bytes 1310744
  17.3 0.0 copy-start
  17.3 0.0 copy-start.2
  17.3 0.0 copy-start.3
  17.3 0.4 shard_map.55.vt_ref
  17.7 0.0 collective-permute-done.4.q_ref
  17.7 0.9 %copy-done = bf16[2,1280,256]{2,1,0:T(8,128)(2,1)S(1)} copy-done((bf16[2,1280,256]{2,1,0:T(8,128)(2,1)S(1)}, bf16[2,1280,256]{2,1,0:T(8,128)(2,1)}, u32[]{:S(2)}) %copy-start) | copy-done | bytes 1310744
  18.7 0.0 copy-done.2
  18.7 0.0 copy-done.3
  18.7 4.1 %shard_map.57 = bf16[4,136,256]{2,1,0:T(8,128)(2,1)S(1)} custom-call(s32[1]{0:T(128)} %bitcast.info_ref, s32[2]{0:T(128)S(1)} %copy-done.2, s32[2]{0:T(128)S(1)} %copy-done.3, bf16[4,256,128]{2,1,0:T(8,128)(2,1)S(1)} %collective-permute-done.4.q_ref, bf16[2,1280,256]{2,1,0:T(8,128)(2,1)S(1)} %copy-done, bf16[2,256,1280]{2,1,0:T(8,128)(2,1)S(1)} %shard_map.55.vt_ref), custom_call_target="tpu_custom_call" | custom-call | flops 671088640 | tf_op jit(solution)/shard_map/pallas_call | solution.py:212
  22.8 0.6 %collective-permute-start.5 = (bf16[4,136,256]{2,1,0:T(8,128)(2,1)S(1)}, bf16[4,136,256]{2,1,0:T(8,128)(2,1)S(1)}, u32[]{:S(2)}, u32[]{:S(2)}) collective-permute-start(bf16[4,136,256]{2,1,0:T(8,128)(2,1)S(1)} %shard_map.57), channel_id=1, source_target_pairs={{0,1},{1,0},{2,3},{3,2},{4,5},{5,4},{6,7},{7,6},{8,9},{9,8},{10,11... | collective-permute-start | bytes 835592 | tf_op jit(solution)/shard_map/ppermute | solution.py:221
  23.3 4.1 %shard_map.56.keep_ref = f32[4,136,256]{2,1,0:T(8,128)S(1)} custom-call(s32[1]{0:T(128)} %bitcast.info_ref, s32[2]{0:T(128)S(1)} %copy-done.2, s32[2]{0:T(128)S(1)} %copy-done.3, bf16[4,256,128]{2,1,0:T(8,128)(2,1)S(1)} %constant_dynamic-update-slice_fusion.q_ref, bf16[2,1280,256]{2,1,0:T(8,128)(2,1)S(1)} %copy-done, bf16[2,256,1280]{2,1,0:T(8,128)(2,1)S(1)} %shard_map.55.vt_ref), custom_call_target="tpu_custom_call" | custom-call | flops 671088640 | tf_op jit(solution)/shard_map/pallas_call | solution.py:212
  27.5 0.0 collective-permute-done.5.refs_0_
  27.5 0.1 shard_map.58
  27.6 1.6 %collective-permute-start.6 = (bf16[4,136,128]{2,1,0:T(8,128)(2,1)S(1)}, bf16[4,136,128]{2,1,0:T(8,128)(2,1)S(1)}, u32[]{:S(2)}, u32[]{:S(2)}) collective-permute-start(bf16[4,136,128]{2,1,0:T(8,128)(2,1)S(1)} %get-tuple-element.12), channel_id=1, source_target_pairs={{0,2},{1,3},{2,0},{3,1},{4,6},{5,7},{6,4},{7,5},{8,10},{9,11},{10,... | collective-permute-start | bytes 417800 | tf_op jit(solution)/shard_map/ppermute | solution.py:237
  29.2 4.1 %collective-permute-done.6.refs_0_ = bf16[4,136,128]{2,1,0:T(8,128)(2,1)S(1)} collective-permute-done((bf16[4,136,128]{2,1,0:T(8,128)(2,1)S(1)}, bf16[4,136,128]{2,1,0:T(8,128)(2,1)S(1)}, u32[]{:S(2)}, u32[]{:S(2)}) %collective-permute-start.6) | collective-permute-done | bytes 139296 | tf_op jit(solution)/shard_map/ppermute | solution.py:237
  33.3 0.2 shard_map.59
  33.5 0.1 collective-permute-start.7
  33.6 2.1 %collective-permute-start.8 = (bf16[136,128]{1,0:T(8,128)(2,1)S(1)}, bf16[136,128]{1,0:T(8,128)(2,1)S(1)}, u32[]{:S(2)}, u32[]{:S(2)}) collective-permute-start(bf16[136,128]{1,0:T(8,128)(2,1)S(1)} %get-tuple-element.15), channel_id=1, source_target_pairs={{0,8},{1,9},{2,10},{3,11},{4,12},{5,13},{6,14},{7,15},{8,0},{9,1},... | collective-permute-start | bytes 104456 | tf_op jit(solution)/shard_map/ppermute | solution.py:237
  35.7 2.3 %collective-permute-start.9 = (bf16[136,128]{1,0:T(8,128)(2,1)S(1)}, bf16[136,128]{1,0:T(8,128)(2,1)S(1)}, u32[]{:S(2)}, u32[]{:S(2)}) collective-permute-start(bf16[136,128]{1,0:T(8,128)(2,1)S(1)} %get-tuple-element.16), channel_id=1, source_target_pairs={{0,12},{1,13},{2,14},{3,15},{4,8},{5,9},{6,10},{7,11},{8,4},{9,5},... | collective-permute-start | bytes 104456 | tf_op jit(solution)/shard_map/ppermute | solution.py:237
  37.9 0.0 collective-permute-done.7.refs_0_
  38.0 0.8 %collective-permute-done.8.refs_1_ = bf16[136,128]{1,0:T(8,128)(2,1)S(1)} collective-permute-done((bf16[136,128]{1,0:T(8,128)(2,1)S(1)}, bf16[136,128]{1,0:T(8,128)(2,1)S(1)}, u32[]{:S(2)}, u32[]{:S(2)}) %collective-permute-start.8) | collective-permute-done | bytes 34848 | tf_op jit(solution)/shard_map/ppermute | solution.py:237
  38.7 2.7 %collective-permute-done.9.refs_2_ = bf16[136,128]{1,0:T(8,128)(2,1)S(1)} collective-permute-done((bf16[136,128]{1,0:T(8,128)(2,1)S(1)}, bf16[136,128]{1,0:T(8,128)(2,1)S(1)}, u32[]{:S(2)}, u32[]{:S(2)}) %collective-permute-start.9) | collective-permute-done | bytes 34848 | tf_op jit(solution)/shard_map/ppermute | solution.py:237
  41.4 0.7 %shard_map.60 = bf16[128,128]{1,0:T(8,128)(2,1)} custom-call(f32[136,128]{1,0:T(8,128)S(1)} %get-tuple-element.13.keep_ref, bf16[136,128]{1,0:T(8,128)(2,1)S(1)} %collective-permute-done.7.refs_0_, bf16[136,128]{1,0:T(8,128)(2,1)S(1)} %collective-permute-done.8.refs_1_, bf16[136,128]{1,0:T(8,128)(2,1)S(1)} %collective-permute-done.9.refs_2_), custom_call_target="tpu_custom_call" | custom-call | tf_op jit(solution)/shard_map/pallas_call | solution.py:238
  (4 shorter events, 0.0 us)
Async XLA Ops:
  0.0 7.2 %collective-permute-start.2 = (bf16[4,32,128]{2,1,0:T(8,128)(2,1)}, bf16[4,32,128]{2,1,0:T(8,128)(2,1)S(1)}, u32[]{:S(2)}, u32[]{:S(2)}) collective-permute-start(bf16[4,32,128]{2,1,0:T(8,128)(2,1)} %bitcast.11), channel_id=1, source_target_pairs={{0,12},{1,13},{2,14},{3,15},{4,8},{5,9},{6,10},{7,11},{8,4},{9,5},... | collective-permute-start | bytes 98312 | tf_op jit(solution)/shard_map/ppermute | solution.py:200
  5.1 5.0 %collective-permute-start.1 = (bf16[4,32,128]{2,1,0:T(8,128)(2,1)}, bf16[4,32,128]{2,1,0:T(8,128)(2,1)S(1)}, u32[]{:S(2)}, u32[]{:S(2)}) collective-permute-start(bf16[4,32,128]{2,1,0:T(8,128)(2,1)} %bitcast.12), channel_id=1, source_target_pairs={{0,8},{1,9},{2,10},{3,11},{4,12},{5,13},{6,14},{7,15},{8,0},{9,1},... | collective-permute-start | bytes 98312 | tf_op jit(solution)/shard_map/ppermute | solution.py:200
  5.1 5.0 %collective-permute-start = (bf16[4,32,128]{2,1,0:T(8,128)(2,1)}, bf16[4,32,128]{2,1,0:T(8,128)(2,1)S(1)}, u32[]{:S(2)}, u32[]{:S(2)}) collective-permute-start(bf16[4,32,128]{2,1,0:T(8,128)(2,1)} %bitcast.13), channel_id=1, source_target_pairs={{0,4},{1,5},{2,6},{3,7},{4,0},{5,1},{6,2},{7,3},{8,12},{9,13},{10,... | collective-permute-start | bytes 98312 | tf_op jit(solution)/shard_map/ppermute | solution.py:200
  10.9 5.0 %collective-permute-start.3 = (bf16[4,128,128]{2,1,0:T(8,128)(2,1)S(1)}, bf16[4,128,128]{2,1,0:T(8,128)(2,1)S(1)}, u32[]{:S(2)}, u32[]{:S(2)}) collective-permute-start(bf16[4,128,128]{2,1,0:T(8,128)(2,1)S(1)} %pad_maximum_fusion), channel_id=1, source_target_pairs={{0,2},{1,3},{2,0},{3,1},{4,6},{5,7},{6,4},{7,5},{8,10},{9,11},{10,... | collective-permute-start | bytes 393224 | tf_op jit(solution)/shard_map/ppermute | solution.py:204
  15.9 1.8 %collective-permute-start.4 = (bf16[4,256,128]{2,1,0:T(8,128)(2,1)S(1)}, bf16[4,256,128]{2,1,0:T(8,128)(2,1)S(1)}, u32[]{:S(2)}, u32[]{:S(2)}) collective-permute-start(bf16[4,256,128]{2,1,0:T(8,128)(2,1)S(1)} %constant_dynamic-update-slice_fusion.q_ref), channel_id=1, source_target_pairs={{0,1},{1,0},{2,3},{3,2},{4,5},{5,4},{6,7},{7,6},{8,9},{9,8},{10,11... | collective-permute-start | bytes 786440 | tf_op jit(solution)/shard_map/ppermute | solution.py:206
  16.0 1.3 %copy-start.1 = (bf16[2,1280,256]{2,1,0:T(8,128)(2,1)S(1)}, bf16[2,1280,256]{2,1,0:T(8,128)(2,1)}, u32[]{:S(2)}) copy-start(bf16[2,1280,256]{2,1,0:T(8,128)(2,1)} %v_ref.1) | copy-start | bytes 3932164
  17.3 1.3 %copy-start = (bf16[2,1280,256]{2,1,0:T(8,128)(2,1)S(1)}, bf16[2,1280,256]{2,1,0:T(8,128)(2,1)}, u32[]{:S(2)}) copy-start(bf16[2,1280,256]{2,1,0:T(8,128)(2,1)} %k_ref.3) | copy-start | bytes 3932164
  17.3 1.3 %copy-start.2 = (s32[2]{0:T(128)S(1)}, s32[2]{0:T(128)}, u32[]{:S(2)}) copy-start(s32[2]{0:T(128)} %len_ref.3) | copy-start | bytes 28
  17.3 1.3 %copy-start.3 = (s32[2]{0:T(128)S(1)}, s32[2]{0:T(128)}, u32[]{:S(2)}) copy-start(s32[2]{0:T(128)} %off_ref.3) | copy-start | bytes 28
  22.8 4.7 %collective-permute-start.5 = (bf16[4,136,256]{2,1,0:T(8,128)(2,1)S(1)}, bf16[4,136,256]{2,1,0:T(8,128)(2,1)S(1)}, u32[]{:S(2)}, u32[]{:S(2)}) collective-permute-start(bf16[4,136,256]{2,1,0:T(8,128)(2,1)S(1)} %shard_map.57), channel_id=1, source_target_pairs={{0,1},{1,0},{2,3},{3,2},{4,5},{5,4},{6,7},{7,6},{8,9},{9,8},{10,11... | collective-permute-start | bytes 835592 | tf_op jit(solution)/shard_map/ppermute | solution.py:221
  27.6 5.7 %collective-permute-start.6 = (bf16[4,136,128]{2,1,0:T(8,128)(2,1)S(1)}, bf16[4,136,128]{2,1,0:T(8,128)(2,1)S(1)}, u32[]{:S(2)}, u32[]{:S(2)}) collective-permute-start(bf16[4,136,128]{2,1,0:T(8,128)(2,1)S(1)} %get-tuple-element.12), channel_id=1, source_target_pairs={{0,2},{1,3},{2,0},{3,1},{4,6},{5,7},{6,4},{7,5},{8,10},{9,11},{10,... | collective-permute-start | bytes 417800 | tf_op jit(solution)/shard_map/ppermute | solution.py:237
  33.5 4.5 %collective-permute-start.7 = (bf16[136,128]{1,0:T(8,128)(2,1)S(1)}, bf16[136,128]{1,0:T(8,128)(2,1)S(1)}, u32[]{:S(2)}, u32[]{:S(2)}) collective-permute-start(bf16[136,128]{1,0:T(8,128)(2,1)S(1)} %get-tuple-element.14), channel_id=1, source_target_pairs={{0,4},{1,5},{2,6},{3,7},{4,0},{5,1},{6,2},{7,3},{8,12},{9,13},{10,... | collective-permute-start | bytes 104456 | tf_op jit(solution)/shard_map/ppermute | solution.py:237
  33.6 5.1 %collective-permute-start.8 = (bf16[136,128]{1,0:T(8,128)(2,1)S(1)}, bf16[136,128]{1,0:T(8,128)(2,1)S(1)}, u32[]{:S(2)}, u32[]{:S(2)}) collective-permute-start(bf16[136,128]{1,0:T(8,128)(2,1)S(1)} %get-tuple-element.15), channel_id=1, source_target_pairs={{0,8},{1,9},{2,10},{3,11},{4,12},{5,13},{6,14},{7,15},{8,0},{9,1},... | collective-permute-start | bytes 104456 | tf_op jit(solution)/shard_map/ppermute | solution.py:237
  35.7 5.7 %collective-permute-start.9 = (bf16[136,128]{1,0:T(8,128)(2,1)S(1)}, bf16[136,128]{1,0:T(8,128)(2,1)S(1)}, u32[]{:S(2)}, u32[]{:S(2)}) collective-permute-start(bf16[136,128]{1,0:T(8,128)(2,1)S(1)} %get-tuple-element.16), channel_id=1, source_target_pairs={{0,12},{1,13},{2,14},{3,15},{4,8},{5,9},{6,10},{7,11},{8,4},{9,5},... | collective-permute-start | bytes 104456 | tf_op jit(solution)/shard_map/ppermute | solution.py:237

commit v2 on v1

--- a/solution.py
+++ b/solution.py
@@ -12,8 +12,10 @@
 HEAD_DIM = 128
 LOW = -1e30
 STAT_ROWS = 8
+PARTS = 5
 
 VMEM = pl.BlockSpec(memory_space=pltpu.VMEM)
+HBM = pl.BlockSpec(memory_space=pltpu.HBM)
 SMEM = pl.BlockSpec(memory_space=pltpu.SMEM)
 
 
@@ -71,44 +73,101 @@
     return num, peak, total
 
 
-def transpose_kernel(v_ref, vt_ref):
-    for micro in range(v_ref.shape[0]):
-        vt_ref[micro] = v_ref[micro].T
-
-
-def attend_kernel(local_rows, lane_masks, send, info_ref, len_ref, off_ref, q_ref, k_ref, vt_ref, out_ref):
-    groups, lanes, _ = q_ref.shape
-    key_count = k_ref.shape[1]
+def prep_kernel(info_ref, len_hbm, off_hbm, q_hbm, k_hbm, v_hbm, q_ref, k_ref, vt_ref, mask_ref, v_ref, len_ref, off_ref, sem):
+    micros, key_count, rows = mask_ref.shape
+    chunk = key_count // PARTS
+
+    def copies(source, target, first):
+        made = []
+        for micro in range(micros):
+            for part in range(PARTS):
+                cut = pl.ds(part * chunk, chunk)
+                made.append(
+                    pltpu.make_async_copy(
+                        source.at[micro, cut], target.at[micro, cut], sem.at[first + len(made)]
+                    )
+                )
+        return made
+
+    own = pltpu.make_async_copy(q_hbm, q_ref, sem.at[2 * micros * PARTS])
+    value_copies = copies(v_hbm, v_ref, 0)
+    key_copies = copies(k_hbm, k_ref, micros * PARTS)
+    bounds = [
+        pltpu.make_async_copy(len_hbm, len_ref, sem.at[2 * micros * PARTS + 1]),
+        pltpu.make_async_copy(off_hbm, off_ref, sem.at[2 * micros * PARTS + 2]),
+    ]
+    for copy in bounds + value_copies + [own] + key_copies:
+        copy.start()
+    for copy in bounds:
+        copy.wait()
+    first = info_ref[0] * key_count
+    row = lax.broadcasted_iota(jnp.int32, (1, rows), 1)
+    key = lax.broadcasted_iota(jnp.int32, (key_count, rows), 0)
+    for micro in range(micros):
+        last = jnp.minimum(off_ref[micro] + row, len_ref[micro] - 1) - first
+        mask_ref[micro] = jnp.where(key <= last, 0.0, LOW).astype(mask_ref.dtype)
+        for head in range(KV_HEADS):
+            vt_ref[micro * KV_HEADS + head, HEAD_DIM:] = jnp.ones((STAT_ROWS, key_count), vt_ref.dtype)
+    for micro in range(micros):
+        for part in range(PARTS):
+            cut = slice(part * chunk, (part + 1) * chunk)
+            value_copies[micro * PARTS + part].wait()
+            for head in range(KV_HEADS):
+                span = slice(head * HEAD_DIM, (head + 1) * HEAD_DIM)
+                vt_ref[micro * KV_HEADS + head, :HEAD_DIM, cut] = v_ref[micro, cut, span].T
+    for copy in [own] + key_copies:
+        copy.wait()
+
+
+def attend_kernel(local_rows, masks, sends, info_ref, *refs):
+    count = len(sends)
+    q_refs, (k_ref, vt_ref, mask_ref), refs = refs[:count], refs[count : count + 3], refs[count + 3 :]
+    out_refs, s_ref = refs[:count], refs[count]
+    groups = q_refs[0].shape[0]
+    block = q_refs[0].shape[1]
+    lanes = block * count
+    table = mask_ref.shape[2]
     me = info_ref[0]
-    width = lanes // len(lane_masks)
-    lane = lax.broadcasted_iota(jnp.int32, (1, lanes), 1)
-    origin = jnp.full((1, lanes), lane_masks[0], jnp.int32)
-    for index, mask in enumerate(lane_masks):
+    width = lanes // len(masks)
+    lane = lax.broadcasted_iota(jnp.int32, (lanes, table), 0)
+    origin = jnp.full((lanes, table), masks[0], jnp.int32)
+    for index, mask in enumerate(masks):
         origin = jnp.where(lane // width == index, mask, origin)
     row = (origin ^ me) * local_rows + lane % local_rows
+    chosen = (row == lax.broadcasted_iota(jnp.int32, (lanes, table), 1)).astype(jnp.float32)
+    chosen = chosen.astype(k_ref.dtype)
     unit = math.log2(math.e) / math.sqrt(HEAD_DIM)
-    key = lax.broadcasted_iota(jnp.int32, (key_count, lanes), 0)
-    for group in range(groups):
+
+    def score(group):
         micro, head = divmod(group, KV_HEADS)
-        last = jnp.minimum(off_ref[micro] + row, len_ref[micro] - 1) - me * key_count
         span = slice(head * HEAD_DIM, (head + 1) * HEAD_DIM)
+        rows = jnp.concatenate([ref[group] for ref in q_refs], axis=0)
         scores = lax.dot_general(
-            k_ref[micro, :, span],
-            q_ref[group],
+            jnp.concatenate([k_ref[micro, :, span], mask_ref[micro]], axis=1),
+            jnp.concatenate([rows, chosen], axis=1),
             (((1,), (1,)), ((), ())),
             preferred_element_type=jnp.float32,
         )
-        scores = jnp.where(key <= last, scores, LOW)
-        top = jnp.max(scores, axis=0, keepdims=True)
-        some = last >= 0
+        s_ref[group % 2] = scores
+        return jnp.max(scores, axis=0, keepdims=True)
+
+    def weigh(group, top):
+        some = top > LOW / 2
         top = jnp.where(some, top, 0.0)
-        weights = jnp.exp2((scores - top) * unit)
-        total = jnp.sum(weights, axis=0, keepdims=True)
-        num = jnp.dot(
-            vt_ref[micro, span, :], weights.astype(jnp.bfloat16), preferred_element_type=jnp.float32
-        )
+        weights = jnp.exp2((s_ref[group % 2] - top) * unit)
+        num = jnp.dot(vt_ref[group], weights.astype(vt_ref.dtype), preferred_element_type=jnp.float32)
+        total = num[HEAD_DIM : HEAD_DIM + 1]
         peak = jnp.where(some, top * unit, LOW)
-        out_ref[group] = packed(num, peak, total) if send else kept(num, peak, total)
+        for index, send in enumerate(sends):
+            cut = slice(index * block, (index + 1) * block)
+            part = (num[:HEAD_DIM, cut], peak[:, cut], total[:, cut])
+            out_refs[index][group] = packed(*part) if send else kept(*part)
+
+    top = score(0)
+    for group in range(groups):
+        following = score(group + 1) if group + 1 < groups else None
+        weigh(group, top)
+        top = following
 
 
 def merge_kernel(ways, received, keep_ref, *refs):
@@ -154,6 +213,12 @@
             send_refs[way - 1][...] = packed(*unkept(block))
 
 
+def join_kernel(send, keep_ref, got_ref, out_ref):
+    for group in range(keep_ref.shape[0]):
+        part = merged([unkept(keep_ref[group]), unpacked(got_ref[group])])
+        out_ref[group] = packed(*part) if send else kept(*part)
+
+
 def final_kernel(keep_ref, *refs):
     got_refs, out_ref = refs[:-1], refs[-1]
     parts = [unkept(keep_ref[...])] + [unpacked(got[...]) for got in got_refs]
@@ -161,66 +226,94 @@
     out_ref[...] = (num / total).T.astype(jnp.bfloat16)
 
 
-def call(kernel, outs, specs, flops=0, nbytes=0, grant=4):
+def call(kernel, outs, specs, flops=0, nbytes=0, grant=4, scratch=()):
     return pl.pallas_call(
         kernel,
         out_shape=outs,
         in_specs=specs,
         out_specs=jax.tree.map(lambda _: VMEM, outs),
+        scratch_shapes=list(scratch),
         cost_estimate=pl.CostEstimate(flops=flops, bytes_accessed=nbytes, transcendentals=0),
         compiler_params=pltpu.CompilerParams(vmem_limit_bytes=grant << 20),
     )
 
 
+def in_hbm(part):
+    return pltpu.with_memory_space_constraint(part, pltpu.HBM)
+
+
 def struct(shape, dtype):
     return jax.ShapeDtypeStruct(shape, dtype)
 
 
-def body(queries, keys, values, lengths, offsets):
+def program(queries, keys, values, lengths, offsets):
     micro_count, local_rows, row_width = queries.shape
     heads = row_width // HEAD_DIM
     share = heads // KV_HEADS
     groups = micro_count * KV_HEADS
     width = share * local_rows
     shards = lax.axis_size("blk")
+    key_count = keys.shape[1]
     masks = digit_masks(shards)
     stacked = HEAD_DIM + STAT_ROWS
+    table = -(-shards * local_rows // HEAD_DIM) * HEAD_DIM
     info = jnp.reshape(lax.axis_index("blk"), (1,)).astype(jnp.int32)
+    low = keys.dtype
+
+    def swap(part, mask):
+        return lax.ppermute(part, "blk", pairs(shards, mask))
 
     own = queries.reshape(micro_count, local_rows, KV_HEADS, share, HEAD_DIM)
     own = own.transpose(0, 2, 3, 1, 4).reshape(groups, width, HEAD_DIM)
-    values_t = call(
-        transpose_kernel, struct((micro_count, values.shape[2], values.shape[1]), values.dtype), [VMEM]
-    )(values)
+    near, keys_in, values_t, seen = call(
+        prep_kernel,
+        [
+            struct(own.shape, low),
+            struct(keys.shape, low),
+            struct((groups, stacked, key_count), low),
+            struct((micro_count, key_count, table), low),
+        ],
+        [SMEM] + [HBM] * 5,
+        nbytes=2 * keys.size * 2,
+        grant=8,
+        scratch=[pltpu.VMEM(values.shape, low), pltpu.SMEM(lengths.shape, jnp.int32), pltpu.SMEM(offsets.shape, jnp.int32), pltpu.SemaphoreType.DMA((2 * micro_count * PARTS + 3,))],
+    )(info, *[in_hbm(part) for part in (lengths, offsets, own, keys, values)])
 
     origin = [0]
-    piece = own
+    source = own
     for level in masks[:1:-1]:
-        piece = jnp.concatenate(
-            [piece] + [lax.ppermute(piece, "blk", pairs(shards, mask)) for mask in level], axis=1
-        )
+        got = [swap(source, mask) for mask in level]
+        near = source = jnp.concatenate([near] + got, axis=1)
         origin = [base ^ mask for mask in [0] + level for base in origin]
-    near = piece
-    far = lax.ppermute(near, "blk", pairs(shards, 2))
-    near_far = jnp.concatenate([near, far], axis=1)
-    across = lax.ppermute(near_far, "blk", pairs(shards, 1))
-    near_origin = origin + [base ^ 2 for base in origin]
-
-    lanes = near_far.shape[1]
-
-    def attend(rows, mask, send):
+    block = near.shape[1]
+
+    def attend(rows, shifts, sends):
+        count = len(rows)
         return call(
-            functools.partial(attend_kernel, local_rows, [base ^ mask for base in near_origin], send),
-            struct((groups, stacked, lanes), jnp.bfloat16 if send else jnp.float32),
-            [SMEM, SMEM, SMEM, VMEM, VMEM, VMEM],
-            flops=4 * groups * lanes * keys.shape[1] * HEAD_DIM,
-            grant=24,
-        )(info, lengths, offsets, rows, keys, values_t)
-
-    sends = attend(across, 1, True)
-    got = [lax.ppermute(sends, "blk", pairs(shards, 1))]
-    keep = attend(near_far, 0, False)
-    for step in range(1, len(masks)):
+            functools.partial(attend_kernel, local_rows, [base ^ shift for shift in shifts for base in origin], sends),
+            [struct((groups, stacked, block), low if send else jnp.float32) for send in sends],
+            [SMEM] + [VMEM] * (count + 3),
+            flops=6 * groups * block * count * key_count * HEAD_DIM,
+            grant=16,
+            scratch=[pltpu.VMEM((2, key_count, block * count), jnp.float32)],
+        )(info, *rows, keys_in, values_t, seen)
+
+    far = swap(near, 2)
+    near_across = swap(near, 1)
+    near_keep, near_send = attend([near, near_across], [0, 1], [False, True])
+    near_got = swap(near_send, 1)
+    far_across = swap(far, 1)
+    far_keep, far_send = attend([far, far_across], [2, 3], [False, True])
+    far_got = swap(far_send, 1)
+    outgoing = call(
+        functools.partial(join_kernel, True), struct((groups, stacked, block), low), [VMEM] * 2
+    )(far_keep, far_got)
+    got = [swap(outgoing, 2)]
+    keep = call(
+        functools.partial(join_kernel, False), struct((groups, stacked, block), jnp.float32), [VMEM] * 2
+    )(near_keep, near_got)
+    lanes = block
+    for step in range(2, len(masks)):
         level = masks[step]
         ways = len(level) + 1
         if step < len(masks) - 1:
@@ -230,13 +323,13 @@
             kernel = merge_repack_kernel
             shape = (stacked, groups * width)
         lanes //= ways
-        outs = [struct(shape, jnp.float32)] + [struct(shape, jnp.bfloat16)] * len(level)
+        outs = [struct(shape, jnp.float32)] + [struct(shape, low)] * len(level)
         keep, *sends = call(
             functools.partial(kernel, ways, len(got)), outs, [VMEM] * (1 + len(got))
         )(keep, *got)
-        got = [lax.ppermute(part, "blk", pairs(shards, mask)) for part, mask in zip(sends, level)]
+        got = [swap(part, mask) for part, mask in zip(sends, level)]
     merged_rows = call(
-        final_kernel, struct((groups * width, HEAD_DIM), jnp.bfloat16), [VMEM] * (1 + len(got))
+        final_kernel, struct((groups * width, HEAD_DIM), low), [VMEM] * (1 + len(got))
     )(keep, *got)
     shaped = merged_rows.reshape(micro_count, KV_HEADS, share, local_rows, HEAD_DIM)
     return shaped.transpose(0, 3, 1, 2, 4).reshape(micro_count, local_rows, row_width)
@@ -244,7 +337,7 @@
 
 def solution(mesh):
     return jax.shard_map(
-        body,
+        program,
         mesh=mesh,
         in_specs=(
             P("group", "blk", None),

time: 42.4 us -> 36 us (0.85)
  local copies, waits for them, and re-layouts: 3.07 us -> 0.03 us
  Pallas kernels: 9.71 us -> 7.66 us
  other arithmetic: 0.77 us -> 0 us
  starting transfers between devices: 13.9 us -> 13.4 us
    unnamed x12 -> x3, local copies, waits for them, and re-layouts: 3.05 us -> 0.02 us
    pallas_call x6 -> x7, Pallas kernels: 9.71 us -> 7.66 us  [the longest x2 4.54 us: attend(): call(functools.partial(attend_kernel, local_rows, [base ^ shift for shift...]
    concatenate x1 -> x0, other arithmetic: 0.77 us -> none  [body(): jnp.concatenate([piece] + [lax.ppermute(piece, 'blk', pairs(shards, mask)...]
    ppermute x10 -> x12, starting transfers between devices: 13.9 us -> 13.4 us  [swap(): return lax.ppermute(part, 'blk', pairs(shards, mask))]
    ppermute x10 -> x12, waiting for transfers between devices: 14.6 us -> 14.6 us  [swap(): return lax.ppermute(part, 'blk', pairs(shards, mask))]
  transfers between devices with their start and end apart: 10 -> 12, of which waited for: 6 -> 7; matrix products, arithmetic and copies ran while one was open for 2% -> 0% of each run, Pallas kernels for 11% -> 19%
where the time goes in v2:
time: 36 us; the launch traced here: 35.8 us
  waiting for transfers between devices  14.6 us (41%)
  starting transfers between devices  13.4 us (37%)
  Pallas kernels  7.66 us (21%)
    ppermute x12, waiting for transfers between devices, swap(): return lax.ppermute(part, 'blk', pairs(shards, mask))  14.6 us
    ppermute x12, starting transfers between devices, swap(): return lax.ppermute(part, 'blk', pairs(shards, mask))  13.4 us
    pallas_call x2, Pallas kernels, attend(): call(functools.partial(attend_kernel, local_rows, [base ^ shift for shift...  4.54 us
    pallas_call x1, Pallas kernels, program(): call(prep_kernel, [struct(own.shape, low), struct(keys.shape, low), struc...  2.02 us
    pallas_call x1, Pallas kernels, program(): call(final_kernel, struct((groups * width, HEAD_DIM), low), [VMEM] * (1 +...  0.75 us
  transfers between devices with their start and end apart: 12, of which 7 were waited for; matrix products, arithmetic and copies ran while one was open for 0% of the time, Pallas kernels for 19%

profile of v2, /device:TPU:0, one launch (start us, length us, event | category | flops | bytes accessed | tf_op | source)
XLA Modules:
  0.0 35.8 jit_solution(3002729335728770464)
XLA Ops:
  0.0 3.1 %collective-permute-start = (bf16[4,32,128]{2,1,0:T(8,128)(2,1)}, bf16[4,32,128]{2,1,0:T(8,128)(2,1)S(1)}, u32[]{:S(2)}, u32[]{:S(2)}) collective-permute-start(bf16[4,32,128]{2,1,0:T(8,128)(2,1)} %bitcast.11), channel_id=1, source_target_pairs={{0,4},{1,5},{2,6},{3,7},{4,0},{5,1},{6,2},{7,3},{8,12},{9,13},{10,... | collective-permute-start | bytes 98312 | tf_op jit(solution)/shard_map/ppermute | solution.py:264
  3.1 2.6 %collective-permute-start.1 = (bf16[4,32,128]{2,1,0:T(8,128)(2,1)}, bf16[4,32,128]{2,1,0:T(8,128)(2,1)S(1)}, u32[]{:S(2)}, u32[]{:S(2)}) collective-permute-start(bf16[4,32,128]{2,1,0:T(8,128)(2,1)} %bitcast.12), channel_id=1, source_target_pairs={{0,8},{1,9},{2,10},{3,11},{4,12},{5,13},{6,14},{7,15},{8,0},{9,1},... | collective-permute-start | bytes 98312 | tf_op jit(solution)/shard_map/ppermute | solution.py:264
  5.6 0.0 collective-permute-start.2
  5.6 2.0 %shard_map.55 = (bf16[4,32,128]{2,1,0:T(8,128)(2,1)S(1)}, bf16[2,1280,256]{2,1,0:T(8,128)(2,1)S(1)}, bf16[4,136,1280]{2,1,0:T(8,128)(2,1)S(1)}, bf16[2,1280,128]{2,1,0:T(8,128)(2,1)S(1)}) custom-call(s32[1]{0:T(128)} %bitcast.info_ref, s32[2]{0:T(128)} %len_hbm.1, s32[2]{0:T(128)} %off_hbm.1, bf16[4,32,128]{2,1,0:T(8,128)(2,1)} %bitcast.14, ...), custom_call_target="tpu_custom_call" | custom-call | bytes 2621440 | tf_op jit(solution)/shard_map/pallas_call | solution.py:268
  7.7 0.0 collective-permute-done
  7.7 1.0 %collective-permute-done.1 = bf16[4,32,128]{2,1,0:T(8,128)(2,1)S(1)} collective-permute-done((bf16[4,32,128]{2,1,0:T(8,128)(2,1)}, bf16[4,32,128]{2,1,0:T(8,128)(2,1)S(1)}, u32[]{:S(2)}, u32[]{:S(2)}) %collective-permute-start.1) | collective-permute-done | bytes 32800 | tf_op jit(solution)/shard_map/ppermute | solution.py:264
  8.7 2.9 %collective-permute-done.2 = bf16[4,32,128]{2,1,0:T(8,128)(2,1)S(1)} collective-permute-done((bf16[4,32,128]{2,1,0:T(8,128)(2,1)}, bf16[4,32,128]{2,1,0:T(8,128)(2,1)S(1)}, u32[]{:S(2)}, u32[]{:S(2)}) %collective-permute-start.2) | collective-permute-done | bytes 32800 | tf_op jit(solution)/shard_map/ppermute | solution.py:264
  11.6 1.5 %collective-permute-start.5 = (bf16[4,128,128]{2,1,0:T(8,128)(2,1)S(1)}, bf16[4,128,128]{2,1,0:T(8,128)(2,1)S(1)}, u32[]{:S(2)}, u32[]{:S(2)}) collective-permute-start(bf16[4,128,128]{2,1,0:T(8,128)(2,1)S(1)} %constant_dynamic-update-slice_fusion.refs_0_), channel_id=1, source_target_pairs={{0,2},{1,3},{2,0},{3,1},{4,6},{5,7},{6,4},{7,5},{8,10},{9,11},{10,... | collective-permute-start | bytes 393224 | tf_op jit(solution)/shard_map/ppermute | solution.py:264
  13.1 3.4 %collective-permute-done.5.refs_0_ = bf16[4,128,128]{2,1,0:T(8,128)(2,1)S(1)} collective-permute-done((bf16[4,128,128]{2,1,0:T(8,128)(2,1)S(1)}, bf16[4,128,128]{2,1,0:T(8,128)(2,1)S(1)}, u32[]{:S(2)}, u32[]{:S(2)}) %collective-permute-start.5) | collective-permute-done | bytes 131104 | tf_op jit(solution)/shard_map/ppermute | solution.py:264
  16.5 0.0 collective-permute-start.6
  16.5 0.5 %collective-permute-start.3 = (bf16[4,128,128]{2,1,0:T(8,128)(2,1)S(1)}, bf16[4,128,128]{2,1,0:T(8,128)(2,1)S(1)}, u32[]{:S(2)}, u32[]{:S(2)}) collective-permute-start(bf16[4,128,128]{2,1,0:T(8,128)(2,1)S(1)} %constant_dynamic-update-slice_fusion.refs_0_), channel_id=1, source_target_pairs={{0,1},{1,0},{2,3},{3,2},{4,5},{5,4},{6,7},{7,6},{8,9},{9,8},{10,11... | collective-permute-start | bytes 393224 | tf_op jit(solution)/shard_map/ppermute | solution.py:264
  17.1 0.8 %collective-permute-done.6.refs_1_ = bf16[4,128,128]{2,1,0:T(8,128)(2,1)S(1)} collective-permute-done((bf16[4,128,128]{2,1,0:T(8,128)(2,1)S(1)}, bf16[4,128,128]{2,1,0:T(8,128)(2,1)S(1)}, u32[]{:S(2)}, u32[]{:S(2)}) %collective-permute-start.6) | collective-permute-done | bytes 131104 | tf_op jit(solution)/shard_map/ppermute | solution.py:264
  17.9 2.3 %shard_map.58 = (f32[4,136,128]{2,1,0:T(8,128)S(1)}, bf16[4,136,128]{2,1,0:T(8,128)(2,1)S(1)}) custom-call(s32[1]{0:T(128)} %bitcast.info_ref, bf16[4,128,128]{2,1,0:T(8,128)(2,1)S(1)} %collective-permute-done.5.refs_0_, bf16[4,128,128]{2,1,0:T(8,128)(2,1)S(1)} %collective-permute-done.6.refs_1_, bf16[2,1280,256]{2,1,0:T(8,128)(2,1)S(1)} %get-tuple-element.18.refs_2_, ...), custom_call_target="tpu_custom_call" | custom-call | flops 1006632960 | tf_op jit(solution)/shard_map/pallas_call | solution.py:292
  20.2 0.2 collective-permute-start.7
  20.4 0.0 collective-permute-done.3.refs_1_
  20.4 2.3 %shard_map.56 = (f32[4,136,128]{2,1,0:T(8,128)S(1)}, bf16[4,136,128]{2,1,0:T(8,128)(2,1)S(1)}) custom-call(s32[1]{0:T(128)} %bitcast.info_ref, bf16[4,128,128]{2,1,0:T(8,128)(2,1)S(1)} %constant_dynamic-update-slice_fusion.refs_0_, bf16[4,128,128]{2,1,0:T(8,128)(2,1)S(1)} %collective-permute-done.3.refs_1_, ...), custom_call_target="tpu_custom_call" | custom-call | flops 1006632960 | tf_op jit(solution)/shard_map/pallas_call | solution.py:292
  22.7 0.4 %collective-permute-start.4 = (bf16[4,136,128]{2,1,0:T(8,128)(2,1)S(1)}, bf16[4,136,128]{2,1,0:T(8,128)(2,1)S(1)}, u32[]{:S(2)}, u32[]{:S(2)}) collective-permute-start(bf16[4,136,128]{2,1,0:T(8,128)(2,1)S(1)} %get-tuple-element.22), channel_id=1, source_target_pairs={{0,1},{1,0},{2,3},{3,2},{4,5},{5,4},{6,7},{7,6},{8,9},{9,8},{10,11... | collective-permute-start | bytes 417800 | tf_op jit(solution)/shard_map/ppermute | solution.py:264
  23.1 0.0 collective-permute-done.7.got_ref
  23.1 0.1 shard_map.59
  23.2 1.6 %collective-permute-start.8 = (bf16[4,136,128]{2,1,0:T(8,128)(2,1)S(1)}, bf16[4,136,128]{2,1,0:T(8,128)(2,1)S(1)}, u32[]{:S(2)}, u32[]{:S(2)}) collective-permute-start(bf16[4,136,128]{2,1,0:T(8,128)(2,1)S(1)} %shard_map.59), channel_id=1, source_target_pairs={{0,2},{1,3},{2,0},{3,1},{4,6},{5,7},{6,4},{7,5},{8,10},{9,11},{10,... | collective-permute-start | bytes 417800 | tf_op jit(solution)/shard_map/ppermute | solution.py:264
  24.8 0.0 collective-permute-done.4.got_ref
  24.8 0.1 shard_map.57.keep_ref
  24.8 4.1 %collective-permute-done.8.refs_0_ = bf16[4,136,128]{2,1,0:T(8,128)(2,1)S(1)} collective-permute-done((bf16[4,136,128]{2,1,0:T(8,128)(2,1)S(1)}, bf16[4,136,128]{2,1,0:T(8,128)(2,1)S(1)}, u32[]{:S(2)}, u32[]{:S(2)}) %collective-permute-start.8) | collective-permute-done | bytes 139296 | tf_op jit(solution)/shard_map/ppermute | solution.py:264
  29.0 0.2 shard_map.60
  29.2 0.1 collective-permute-start.10
  29.3 1.3 %collective-permute-start.11 = (bf16[136,128]{1,0:T(8,128)(2,1)S(1)}, bf16[136,128]{1,0:T(8,128)(2,1)S(1)}, u32[]{:S(2)}, u32[]{:S(2)}) collective-permute-start(bf16[136,128]{1,0:T(8,128)(2,1)S(1)} %get-tuple-element.28), channel_id=1, source_target_pairs={{0,12},{1,13},{2,14},{3,15},{4,8},{5,9},{6,10},{7,11},{8,4},{9,5},... | collective-permute-start | bytes 104456 | tf_op jit(solution)/shard_map/ppermute | solution.py:264
  30.6 2.1 %collective-permute-start.9 = (bf16[136,128]{1,0:T(8,128)(2,1)S(1)}, bf16[136,128]{1,0:T(8,128)(2,1)S(1)}, u32[]{:S(2)}, u32[]{:S(2)}) collective-permute-start(bf16[136,128]{1,0:T(8,128)(2,1)S(1)} %get-tuple-element.26), channel_id=1, source_target_pairs={{0,4},{1,5},{2,6},{3,7},{4,0},{5,1},{6,2},{7,3},{8,12},{9,13},{10,... | collective-permute-start | bytes 104456 | tf_op jit(solution)/shard_map/ppermute | solution.py:264
  32.8 1.3 %collective-permute-done.10.refs_1_ = bf16[136,128]{1,0:T(8,128)(2,1)S(1)} collective-permute-done((bf16[136,128]{1,0:T(8,128)(2,1)S(1)}, bf16[136,128]{1,0:T(8,128)(2,1)S(1)}, u32[]{:S(2)}, u32[]{:S(2)}) %collective-permute-start.10) | collective-permute-done | bytes 34848 | tf_op jit(solution)/shard_map/ppermute | solution.py:264
  34.1 1.0 %collective-permute-done.11.refs_2_ = bf16[136,128]{1,0:T(8,128)(2,1)S(1)} collective-permute-done((bf16[136,128]{1,0:T(8,128)(2,1)S(1)}, bf16[136,128]{1,0:T(8,128)(2,1)S(1)}, u32[]{:S(2)}, u32[]{:S(2)}) %collective-permute-start.11) | collective-permute-done | bytes 34848 | tf_op jit(solution)/shard_map/ppermute | solution.py:264
  35.1 0.0 collective-permute-done.9.refs_0_
  35.1 0.7 %shard_map.61 = bf16[128,128]{1,0:T(8,128)(2,1)} custom-call(f32[136,128]{1,0:T(8,128)S(1)} %get-tuple-element.25.keep_ref, bf16[136,128]{1,0:T(8,128)(2,1)S(1)} %collective-permute-done.9.refs_0_, bf16[136,128]{1,0:T(8,128)(2,1)S(1)} %collective-permute-done.10.refs_1_, bf16[136,128]{1,0:T(8,128)(2,1)S(1)} %collective-permute-done.11.refs_2_), custom_call_target="tpu_custom_call" | custom-call | tf_op jit(solution)/shard_map/pallas_call | solution.py:331
  (4 shorter events, 0.0 us)
Async XLA Ops:
  0.0 7.7 %collective-permute-start = (bf16[4,32,128]{2,1,0:T(8,128)(2,1)}, bf16[4,32,128]{2,1,0:T(8,128)(2,1)S(1)}, u32[]{:S(2)}, u32[]{:S(2)}) collective-permute-start(bf16[4,32,128]{2,1,0:T(8,128)(2,1)} %bitcast.11), channel_id=1, source_target_pairs={{0,4},{1,5},{2,6},{3,7},{4,0},{5,1},{6,2},{7,3},{8,12},{9,13},{10,... | collective-permute-start | bytes 98312 | tf_op jit(solution)/shard_map/ppermute | solution.py:264
  3.1 5.6 %collective-permute-start.1 = (bf16[4,32,128]{2,1,0:T(8,128)(2,1)}, bf16[4,32,128]{2,1,0:T(8,128)(2,1)S(1)}, u32[]{:S(2)}, u32[]{:S(2)}) collective-permute-start(bf16[4,32,128]{2,1,0:T(8,128)(2,1)} %bitcast.12), channel_id=1, source_target_pairs={{0,8},{1,9},{2,10},{3,11},{4,12},{5,13},{6,14},{7,15},{8,0},{9,1},... | collective-permute-start | bytes 98312 | tf_op jit(solution)/shard_map/ppermute | solution.py:264
  5.6 5.9 %collective-permute-start.2 = (bf16[4,32,128]{2,1,0:T(8,128)(2,1)}, bf16[4,32,128]{2,1,0:T(8,128)(2,1)S(1)}, u32[]{:S(2)}, u32[]{:S(2)}) collective-permute-start(bf16[4,32,128]{2,1,0:T(8,128)(2,1)} %bitcast.13), channel_id=1, source_target_pairs={{0,12},{1,13},{2,14},{3,15},{4,8},{5,9},{6,10},{7,11},{8,4},{9,5},... | collective-permute-start | bytes 98312 | tf_op jit(solution)/shard_map/ppermute | solution.py:264
  11.6 5.0 %collective-permute-start.5 = (bf16[4,128,128]{2,1,0:T(8,128)(2,1)S(1)}, bf16[4,128,128]{2,1,0:T(8,128)(2,1)S(1)}, u32[]{:S(2)}, u32[]{:S(2)}) collective-permute-start(bf16[4,128,128]{2,1,0:T(8,128)(2,1)S(1)} %constant_dynamic-update-slice_fusion.refs_0_), channel_id=1, source_target_pairs={{0,2},{1,3},{2,0},{3,1},{4,6},{5,7},{6,4},{7,5},{8,10},{9,11},{10,... | collective-permute-start | bytes 393224 | tf_op jit(solution)/shard_map/ppermute | solution.py:264
  16.5 1.3 %collective-permute-start.6 = (bf16[4,128,128]{2,1,0:T(8,128)(2,1)S(1)}, bf16[4,128,128]{2,1,0:T(8,128)(2,1)S(1)}, u32[]{:S(2)}, u32[]{:S(2)}) collective-permute-start(bf16[4,128,128]{2,1,0:T(8,128)(2,1)S(1)} %collective-permute-done.5.refs_0_), channel_id=1, source_target_pairs={{0,1},{1,0},{2,3},{3,2},{4,5},{5,4},{6,7},{7,6},{8,9},{9,8},{10,11... | collective-permute-start | bytes 393224 | tf_op jit(solution)/shard_map/ppermute | solution.py:264
  16.5 3.8 %collective-permute-start.3 = (bf16[4,128,128]{2,1,0:T(8,128)(2,1)S(1)}, bf16[4,128,128]{2,1,0:T(8,128)(2,1)S(1)}, u32[]{:S(2)}, u32[]{:S(2)}) collective-permute-start(bf16[4,128,128]{2,1,0:T(8,128)(2,1)S(1)} %constant_dynamic-update-slice_fusion.refs_0_), channel_id=1, source_target_pairs={{0,1},{1,0},{2,3},{3,2},{4,5},{5,4},{6,7},{7,6},{8,9},{9,8},{10,11... | collective-permute-start | bytes 393224 | tf_op jit(solution)/shard_map/ppermute | solution.py:264
  20.2 2.9 %collective-permute-start.7 = (bf16[4,136,128]{2,1,0:T(8,128)(2,1)S(1)}, bf16[4,136,128]{2,1,0:T(8,128)(2,1)S(1)}, u32[]{:S(2)}, u32[]{:S(2)}) collective-permute-start(bf16[4,136,128]{2,1,0:T(8,128)(2,1)S(1)} %get-tuple-element.24), channel_id=1, source_target_pairs={{0,1},{1,0},{2,3},{3,2},{4,5},{5,4},{6,7},{7,6},{8,9},{9,8},{10,11... | collective-permute-start | bytes 417800 | tf_op jit(solution)/shard_map/ppermute | solution.py:264
  22.7 2.1 %collective-permute-start.4 = (bf16[4,136,128]{2,1,0:T(8,128)(2,1)S(1)}, bf16[4,136,128]{2,1,0:T(8,128)(2,1)S(1)}, u32[]{:S(2)}, u32[]{:S(2)}) collective-permute-start(bf16[4,136,128]{2,1,0:T(8,128)(2,1)S(1)} %get-tuple-element.22), channel_id=1, source_target_pairs={{0,1},{1,0},{2,3},{3,2},{4,5},{5,4},{6,7},{7,6},{8,9},{9,8},{10,11... | collective-permute-start | bytes 417800 | tf_op jit(solution)/shard_map/ppermute | solution.py:264
  23.2 5.8 %collective-permute-start.8 = (bf16[4,136,128]{2,1,0:T(8,128)(2,1)S(1)}, bf16[4,136,128]{2,1,0:T(8,128)(2,1)S(1)}, u32[]{:S(2)}, u32[]{:S(2)}) collective-permute-start(bf16[4,136,128]{2,1,0:T(8,128)(2,1)S(1)} %shard_map.59), channel_id=1, source_target_pairs={{0,2},{1,3},{2,0},{3,1},{4,6},{5,7},{6,4},{7,5},{8,10},{9,11},{10,... | collective-permute-start | bytes 417800 | tf_op jit(solution)/shard_map/ppermute | solution.py:264
  29.2 4.9 %collective-permute-start.10 = (bf16[136,128]{1,0:T(8,128)(2,1)S(1)}, bf16[136,128]{1,0:T(8,128)(2,1)S(1)}, u32[]{:S(2)}, u32[]{:S(2)}) collective-permute-start(bf16[136,128]{1,0:T(8,128)(2,1)S(1)} %get-tuple-element.27), channel_id=1, source_target_pairs={{0,8},{1,9},{2,10},{3,11},{4,12},{5,13},{6,14},{7,15},{8,0},{9,1},... | collective-permute-start | bytes 104456 | tf_op jit(solution)/shard_map/ppermute | solution.py:264
  29.3 5.8 %collective-permute-start.11 = (bf16[136,128]{1,0:T(8,128)(2,1)S(1)}, bf16[136,128]{1,0:T(8,128)(2,1)S(1)}, u32[]{:S(2)}, u32[]{:S(2)}) collective-permute-start(bf16[136,128]{1,0:T(8,128)(2,1)S(1)} %get-tuple-element.28), channel_id=1, source_target_pairs={{0,12},{1,13},{2,14},{3,15},{4,8},{5,9},{6,10},{7,11},{8,4},{9,5},... | collective-permute-start | bytes 104456 | tf_op jit(solution)/shard_map/ppermute | solution.py:264
  30.6 4.5 %collective-permute-start.9 = (bf16[136,128]{1,0:T(8,128)(2,1)S(1)}, bf16[136,128]{1,0:T(8,128)(2,1)S(1)}, u32[]{:S(2)}, u32[]{:S(2)}) collective-permute-start(bf16[136,128]{1,0:T(8,128)(2,1)S(1)} %get-tuple-element.26), channel_id=1, source_target_pairs={{0,4},{1,5},{2,6},{3,7},{4,0},{5,1},{6,2},{7,3},{8,12},{9,13},{10,... | collective-permute-start | bytes 104456 | tf_op jit(solution)/shard_map/ppermute | solution.py:264

commit v3 on v2

--- a/solution.py
+++ b/solution.py
@@ -119,7 +119,7 @@
         copy.wait()
 
 
-def attend_kernel(local_rows, masks, sends, info_ref, *refs):
+def attend_kernel(local_rows, masks, sends, base, info_ref, *refs):
     count = len(sends)
     q_refs, (k_ref, vt_ref, mask_ref), refs = refs[:count], refs[count : count + 3], refs[count + 3 :]
     out_refs, s_ref = refs[:count], refs[count]
@@ -139,7 +139,7 @@
     unit = math.log2(math.e) / math.sqrt(HEAD_DIM)
 
     def score(group):
-        micro, head = divmod(group, KV_HEADS)
+        micro, head = divmod(base + group, KV_HEADS)
         span = slice(head * HEAD_DIM, (head + 1) * HEAD_DIM)
         rows = jnp.concatenate([ref[group] for ref in q_refs], axis=0)
         scores = lax.dot_general(
@@ -155,7 +155,7 @@
         some = top > LOW / 2
         top = jnp.where(some, top, 0.0)
         weights = jnp.exp2((s_ref[group % 2] - top) * unit)
-        num = jnp.dot(vt_ref[group], weights.astype(vt_ref.dtype), preferred_element_type=jnp.float32)
+        num = jnp.dot(vt_ref[base + group], weights.astype(vt_ref.dtype), preferred_element_type=jnp.float32)
         total = num[HEAD_DIM : HEAD_DIM + 1]
         peak = jnp.where(some, top * unit, LOW)
         for index, send in enumerate(sends):
@@ -287,31 +287,40 @@
         origin = [base ^ mask for mask in [0] + level for base in origin]
     block = near.shape[1]
 
-    def attend(rows, shifts, sends):
-        count = len(rows)
+    def attend(rows, shifts, sends, base=0):
+        count, held = len(rows), rows[0].shape[0]
         return call(
-            functools.partial(attend_kernel, local_rows, [base ^ shift for shift in shifts for base in origin], sends),
-            [struct((groups, stacked, block), low if send else jnp.float32) for send in sends],
+            functools.partial(
+                attend_kernel,
+                local_rows,
+                [mask ^ shift for shift in shifts for mask in origin],
+                sends,
+                base,
+            ),
+            [struct((held, stacked, block), low if send else jnp.float32) for send in sends],
             [SMEM] + [VMEM] * (count + 3),
-            flops=6 * groups * block * count * key_count * HEAD_DIM,
+            flops=6 * held * block * count * key_count * HEAD_DIM,
             grant=16,
             scratch=[pltpu.VMEM((2, key_count, block * count), jnp.float32)],
         )(info, *rows, keys_in, values_t, seen)
 
-    far = swap(near, 2)
+    def join(send, keep, got):
+        outs = struct(keep.shape, low if send else jnp.float32)
+        return call(functools.partial(join_kernel, send), outs, [VMEM] * 2)(keep, got)
+
+    micros = range(micro_count)
     near_across = swap(near, 1)
+    fars = [swap(near[m * KV_HEADS : (m + 1) * KV_HEADS], 2) for m in micros]
     near_keep, near_send = attend([near, near_across], [0, 1], [False, True])
     near_got = swap(near_send, 1)
-    far_across = swap(far, 1)
-    far_keep, far_send = attend([far, far_across], [2, 3], [False, True])
-    far_got = swap(far_send, 1)
-    outgoing = call(
-        functools.partial(join_kernel, True), struct((groups, stacked, block), low), [VMEM] * 2
-    )(far_keep, far_got)
-    got = [swap(outgoing, 2)]
-    keep = call(
-        functools.partial(join_kernel, False), struct((groups, stacked, block), jnp.float32), [VMEM] * 2
-    )(near_keep, near_got)
+    got = []
+    for m in micros:
+        across = swap(fars[m], 1)
+        far_keep, far_send = attend([fars[m], across], [2, 3], [False, True], m * KV_HEADS)
+        far_got = swap(far_send, 1)
+        got.append(swap(join(True, far_keep, far_got), 2))
+    got = [jnp.concatenate(got, axis=0)]
+    keep = join(False, near_keep, near_got)
     lanes = block
     for step in range(2, len(masks)):
         level = masks[step]

time: 36 us -> 37.4 us (1.039)
  starting transfers between devices: 13.4 us -> 15.8 us
  waiting for transfers between devices: 14.6 us -> 13.2 us
  Pallas kernels: 7.66 us -> 8.08 us
    ppermute x12 -> x16, starting transfers between devices: 13.4 us -> 15.8 us  [swap(): return lax.ppermute(part, 'blk', pairs(shards, mask))]
    ppermute x12 -> x16, waiting for transfers between devices: 14.6 us -> 13.2 us  [swap(): return lax.ppermute(part, 'blk', pairs(shards, mask))]
    pallas_call x4 -> x6, Pallas kernels: 4.68 us -> 5.09 us  [the longest x3 4.94 us: attend(): call(functools.partial(attend_kernel, local_rows, [mask ^ shift for shift...]
  transfers between devices with their start and end apart: 12 -> 16, of which waited for: 7 -> 8; matrix products, arithmetic and copies ran while one was open for 0% -> 0% of each run, Pallas kernels for 19% -> 19%
where the time goes in v3:
time: 37.4 us; the launch traced here: 37.3 us
  starting transfers between devices  15.8 us (42%)
  waiting for transfers between devices  13.2 us (35%)
  Pallas kernels  8.08 us (22%)
    ppermute x16, starting transfers between devices, swap(): return lax.ppermute(part, 'blk', pairs(shards, mask))  15.8 us
    ppermute x16, waiting for transfers between devices, swap(): return lax.ppermute(part, 'blk', pairs(shards, mask))  13.2 us
    pallas_call x3, Pallas kernels, attend(): call(functools.partial(attend_kernel, local_rows, [mask ^ shift for shift...  4.94 us
    pallas_call x1, Pallas kernels, program(): call(prep_kernel, [struct(own.shape, low), struct(keys.shape, low), struc...  2.01 us
  transfers between devices with their start and end apart: 16, of which 8 were waited for; matrix products, arithmetic and copies ran while one was open for 0% of the time, Pallas kernels for 19%

profile of v3, /device:TPU:0, one launch (start us, length us, event | category | flops | bytes accessed | tf_op | source)
XLA Modules:
  0.0 37.3 jit_solution(11638658167751580643)
XLA Ops:
  0.0 5.1 %collective-permute-start.2 = (bf16[4,32,128]{2,1,0:T(8,128)(2,1)}, bf16[4,32,128]{2,1,0:T(8,128)(2,1)S(1)}, u32[]{:S(2)}, u32[]{:S(2)}) collective-permute-start(bf16[4,32,128]{2,1,0:T(8,128)(2,1)} %bitcast.11), channel_id=1, source_target_pairs={{0,12},{1,13},{2,14},{3,15},{4,8},{5,9},{6,10},{7,11},{8,4},{9,5},... | collective-permute-start | bytes 98312 | tf_op jit(solution)/shard_map/ppermute | solution.py:264
  5.1 0.0 collective-permute-start.1
  5.1 0.6 %collective-permute-start = (bf16[4,32,128]{2,1,0:T(8,128)(2,1)}, bf16[4,32,128]{2,1,0:T(8,128)(2,1)S(1)}, u32[]{:S(2)}, u32[]{:S(2)}) collective-permute-start(bf16[4,32,128]{2,1,0:T(8,128)(2,1)} %bitcast.13), channel_id=1, source_target_pairs={{0,4},{1,5},{2,6},{3,7},{4,0},{5,1},{6,2},{7,3},{8,12},{9,13},{10,... | collective-permute-start | bytes 98312 | tf_op jit(solution)/shard_map/ppermute | solution.py:264
  5.6 2.0 %shard_map.55 = (bf16[4,32,128]{2,1,0:T(8,128)(2,1)S(1)}, bf16[2,1280,256]{2,1,0:T(8,128)(2,1)S(1)}, bf16[4,136,1280]{2,1,0:T(8,128)(2,1)S(1)}, bf16[2,1280,128]{2,1,0:T(8,128)(2,1)S(1)}) custom-call(s32[1]{0:T(128)} %bitcast.info_ref, s32[2]{0:T(128)} %len_hbm.1, s32[2]{0:T(128)} %off_hbm.1, bf16[4,32,128]{2,1,0:T(8,128)(2,1)} %bitcast.14, ...), custom_call_target="tpu_custom_call" | custom-call | bytes 2621440 | tf_op jit(solution)/shard_map/pallas_call | solution.py:268
  7.7 1.5 %collective-permute-done = bf16[4,32,128]{2,1,0:T(8,128)(2,1)S(1)} collective-permute-done((bf16[4,32,128]{2,1,0:T(8,128)(2,1)}, bf16[4,32,128]{2,1,0:T(8,128)(2,1)S(1)}, u32[]{:S(2)}, u32[]{:S(2)}) %collective-permute-start) | collective-permute-done | bytes 32800 | tf_op jit(solution)/shard_map/ppermute | solution.py:264
  9.2 0.9 %collective-permute-done.1 = bf16[4,32,128]{2,1,0:T(8,128)(2,1)S(1)} collective-permute-done((bf16[4,32,128]{2,1,0:T(8,128)(2,1)}, bf16[4,32,128]{2,1,0:T(8,128)(2,1)S(1)}, u32[]{:S(2)}, u32[]{:S(2)}) %collective-permute-start.1) | collective-permute-done | bytes 32800 | tf_op jit(solution)/shard_map/ppermute | solution.py:264
  10.1 0.0 collective-permute-done.2
  10.2 1.6 %collective-permute-start.5 = (bf16[2,128,128]{2,1,0:T(8,128)(2,1)S(1)}, bf16[2,128,128]{2,1,0:T(8,128)(2,1)S(1)}, u32[]{:S(2)}, u32[]{:S(2)}) collective-permute-start(bf16[2,128,128]{2,1,0:T(8,128)(2,1)S(1)} %get-tuple-element.33), channel_id=1, source_target_pairs={{0,2},{1,3},{2,0},{3,1},{4,6},{5,7},{6,4},{7,5},{8,10},{9,11},{10,... | collective-permute-start | bytes 196616 | tf_op jit(solution)/shard_map/ppermute | solution.py:264
  11.7 0.0 collective-permute-start.3
  11.7 0.5 %collective-permute-start.9 = (bf16[2,128,128]{2,1,0:T(8,128)(2,1)S(1)}, bf16[2,128,128]{2,1,0:T(8,128)(2,1)S(1)}, u32[]{:S(2)}, u32[]{:S(2)}) collective-permute-start(bf16[2,128,128]{2,1,0:T(8,128)(2,1)S(1)} %get-tuple-element.34), channel_id=1, source_target_pairs={{0,2},{1,3},{2,0},{3,1},{4,6},{5,7},{6,4},{7,5},{8,10},{9,11},{10,... | collective-permute-start | bytes 196616 | tf_op jit(solution)/shard_map/ppermute | solution.py:264
  12.2 2.2 %collective-permute-done.5.refs_0_ = bf16[2,128,128]{2,1,0:T(8,128)(2,1)S(1)} collective-permute-done((bf16[2,128,128]{2,1,0:T(8,128)(2,1)S(1)}, bf16[2,128,128]{2,1,0:T(8,128)(2,1)S(1)}, u32[]{:S(2)}, u32[]{:S(2)}) %collective-permute-start.5) | collective-permute-done | bytes 65568 | tf_op jit(solution)/shard_map/ppermute | solution.py:264
  14.5 0.0 collective-permute-start.6
  14.5 1.8 %collective-permute-done.9.refs_0_ = bf16[2,128,128]{2,1,0:T(8,128)(2,1)S(1)} collective-permute-done((bf16[2,128,128]{2,1,0:T(8,128)(2,1)S(1)}, bf16[2,128,128]{2,1,0:T(8,128)(2,1)S(1)}, u32[]{:S(2)}, u32[]{:S(2)}) %collective-permute-start.9) | collective-permute-done | bytes 65568 | tf_op jit(solution)/shard_map/ppermute | solution.py:264
  16.2 0.0 collective-permute-start.10
  16.2 0.0 collective-permute-done.6.refs_1_
  16.3 1.3 %shard_map.58 = (f32[2,136,128]{2,1,0:T(8,128)S(1)}, bf16[2,136,128]{2,1,0:T(8,128)(2,1)S(1)}) custom-call(s32[1]{0:T(128)} %bitcast.info_ref, bf16[2,128,128]{2,1,0:T(8,128)(2,1)S(1)} %collective-permute-done.5.refs_0_, bf16[2,128,128]{2,1,0:T(8,128)(2,1)S(1)} %collective-permute-done.6.refs_1_, bf16[2,1280,256]{2,1,0:T(8,128)(2,1)S(1)} %get-tuple-element.20.refs_2_, ...), custom_call_target="tpu_custom_call" | custom-call | flops 503316480 | tf_op jit(solution)/shard_map/pallas_call | solution.py:292
  17.6 0.6 %collective-permute-start.7 = (bf16[2,136,128]{2,1,0:T(8,128)(2,1)S(1)}, bf16[2,136,128]{2,1,0:T(8,128)(2,1)S(1)}, u32[]{:S(2)}, u32[]{:S(2)}) collective-permute-start(bf16[2,136,128]{2,1,0:T(8,128)(2,1)S(1)} %get-tuple-element.26), channel_id=1, source_target_pairs={{0,1},{1,0},{2,3},{3,2},{4,5},{5,4},{6,7},{7,6},{8,9},{9,8},{10,11... | collective-permute-start | bytes 208904 | tf_op jit(solution)/shard_map/ppermute | solution.py:264
  18.2 0.0 collective-permute-done.3.refs_1_
  18.2 2.3 %shard_map.56 = (f32[4,136,128]{2,1,0:T(8,128)S(1)}, bf16[4,136,128]{2,1,0:T(8,128)(2,1)S(1)}) custom-call(s32[1]{0:T(128)} %bitcast.info_ref, bf16[4,128,128]{2,1,0:T(8,128)(2,1)S(1)} %constant_dynamic-update-slice_fusion.refs_0_, bf16[4,128,128]{2,1,0:T(8,128)(2,1)S(1)} %collective-permute-done.3.refs_1_, ...), custom_call_target="tpu_custom_call" | custom-call | flops 1006632960 | tf_op jit(solution)/shard_map/pallas_call | solution.py:292
  20.4 0.1 collective-permute-start.4
  20.5 0.0 collective-permute-done.10.refs_1_
  20.5 1.3 %shard_map.60 = (f32[2,136,128]{2,1,0:T(8,128)S(1)}, bf16[2,136,128]{2,1,0:T(8,128)(2,1)S(1)}) custom-call(s32[1]{0:T(128)} %bitcast.info_ref, bf16[2,128,128]{2,1,0:T(8,128)(2,1)S(1)} %collective-permute-done.9.refs_0_, bf16[2,128,128]{2,1,0:T(8,128)(2,1)S(1)} %collective-permute-done.10.refs_1_, bf16[2,1280,256]{2,1,0:T(8,128)(2,1)S(1)} %get-tuple-element.20.refs_2_, ...), custom_call_target="tpu_custom_call" | custom-call | flops 503316480 | tf_op jit(solution)/shard_map/pallas_call | solution.py:292
  21.9 0.6 %collective-permute-start.11 = (bf16[2,136,128]{2,1,0:T(8,128)(2,1)S(1)}, bf16[2,136,128]{2,1,0:T(8,128)(2,1)S(1)}, u32[]{:S(2)}, u32[]{:S(2)}) collective-permute-start(bf16[2,136,128]{2,1,0:T(8,128)(2,1)S(1)} %get-tuple-element.28), channel_id=1, source_target_pairs={{0,1},{1,0},{2,3},{3,2},{4,5},{5,4},{6,7},{7,6},{8,9},{9,8},{10,11... | collective-permute-start | bytes 208904 | tf_op jit(solution)/shard_map/ppermute | solution.py:264
  22.4 0.0 collective-permute-done.7.got_ref
  22.5 1.4 %collective-permute-start.8 = (bf16[2,136,128]{2,1,0:T(8,128)(2,1)S(1)}, bf16[2,136,128]{2,1,0:T(8,128)(2,1)S(1)}, u32[]{:S(2)}, u32[]{:S(2)}) collective-permute-start(bf16[2,136,128]{2,1,0:T(8,128)(2,1)S(1)} %shard_map.59), channel_id=1, source_target_pairs={{0,2},{1,3},{2,0},{3,1},{4,6},{5,7},{6,4},{7,5},{8,10},{9,11},{10,... | collective-permute-start | bytes 208904 | tf_op jit(solution)/shard_map/ppermute | solution.py:264
  23.9 0.0 collective-permute-done.11.got_ref
  23.9 1.1 %collective-permute-start.12 = (bf16[2,136,128]{2,1,0:T(8,128)(2,1)S(1)}, bf16[2,136,128]{2,1,0:T(8,128)(2,1)S(1)}, u32[]{:S(2)}, u32[]{:S(2)}) collective-permute-start(bf16[2,136,128]{2,1,0:T(8,128)(2,1)S(1)} %shard_map.61), channel_id=1, source_target_pairs={{0,2},{1,3},{2,0},{3,1},{4,6},{5,7},{6,4},{7,5},{8,10},{9,11},{10,... | collective-permute-start | bytes 208904 | tf_op jit(solution)/shard_map/ppermute | solution.py:264
  25.0 0.0 collective-permute-done.4.got_ref
  25.0 0.1 shard_map.57.keep_ref
  25.0 2.0 %collective-permute-done.8 = bf16[2,136,128]{2,1,0:T(8,128)(2,1)S(1)} collective-permute-done((bf16[2,136,128]{2,1,0:T(8,128)(2,1)S(1)}, bf16[2,136,128]{2,1,0:T(8,128)(2,1)S(1)}, u32[]{:S(2)}, u32[]{:S(2)}) %collective-permute-start.8) | collective-permute-done | bytes 69664 | tf_op jit(solution)/shard_map/ppermute | solution.py:264
  27.1 1.3 %collective-permute-done.12 = bf16[2,136,128]{2,1,0:T(8,128)(2,1)S(1)} collective-permute-done((bf16[2,136,128]{2,1,0:T(8,128)(2,1)S(1)}, bf16[2,136,128]{2,1,0:T(8,128)(2,1)S(1)}, u32[]{:S(2)}, u32[]{:S(2)}) %collective-permute-start.12) | collective-permute-done | bytes 69664 | tf_op jit(solution)/shard_map/ppermute | solution.py:264
  28.4 0.2 shard_map.62
  28.6 0.1 collective-permute-start.13
  28.7 2.1 %collective-permute-start.14 = (bf16[136,128]{1,0:T(8,128)(2,1)S(1)}, bf16[136,128]{1,0:T(8,128)(2,1)S(1)}, u32[]{:S(2)}, u32[]{:S(2)}) collective-permute-start(bf16[136,128]{1,0:T(8,128)(2,1)S(1)} %get-tuple-element.31), channel_id=1, source_target_pairs={{0,8},{1,9},{2,10},{3,11},{4,12},{5,13},{6,14},{7,15},{8,0},{9,1},... | collective-permute-start | bytes 104456 | tf_op jit(solution)/shard_map/ppermute | solution.py:264
  30.8 2.3 %collective-permute-start.15 = (bf16[136,128]{1,0:T(8,128)(2,1)S(1)}, bf16[136,128]{1,0:T(8,128)(2,1)S(1)}, u32[]{:S(2)}, u32[]{:S(2)}) collective-permute-start(bf16[136,128]{1,0:T(8,128)(2,1)S(1)} %get-tuple-element.32), channel_id=1, source_target_pairs={{0,12},{1,13},{2,14},{3,15},{4,8},{5,9},{6,10},{7,11},{8,4},{9,5},... | collective-permute-start | bytes 104456 | tf_op jit(solution)/shard_map/ppermute | solution.py:264
  33.1 0.0 collective-permute-done.13.refs_0_
  33.1 0.5 %collective-permute-done.14.refs_1_ = bf16[136,128]{1,0:T(8,128)(2,1)S(1)} collective-permute-done((bf16[136,128]{1,0:T(8,128)(2,1)S(1)}, bf16[136,128]{1,0:T(8,128)(2,1)S(1)}, u32[]{:S(2)}, u32[]{:S(2)}) %collective-permute-start.14) | collective-permute-done | bytes 34848 | tf_op jit(solution)/shard_map/ppermute | solution.py:264
  33.6 3.0 %collective-permute-done.15.refs_2_ = bf16[136,128]{1,0:T(8,128)(2,1)S(1)} collective-permute-done((bf16[136,128]{1,0:T(8,128)(2,1)S(1)}, bf16[136,128]{1,0:T(8,128)(2,1)S(1)}, u32[]{:S(2)}, u32[]{:S(2)}) %collective-permute-start.15) | collective-permute-done | bytes 34848 | tf_op jit(solution)/shard_map/ppermute | solution.py:264
  36.5 0.7 %shard_map.63 = bf16[128,128]{1,0:T(8,128)(2,1)} custom-call(f32[136,128]{1,0:T(8,128)S(1)} %get-tuple-element.29.keep_ref, bf16[136,128]{1,0:T(8,128)(2,1)S(1)} %collective-permute-done.13.refs_0_, bf16[136,128]{1,0:T(8,128)(2,1)S(1)} %collective-permute-done.14.refs_1_, bf16[136,128]{1,0:T(8,128)(2,1)S(1)} %collective-permute-done.15.refs_2_), custom_call_target="tpu_custom_call" | custom-call | tf_op jit(solution)/shard_map/pallas_call | solution.py:340
  (8 shorter events, 0.2 us)
Async XLA Ops:
  0.0 10.1 %collective-permute-start.2 = (bf16[4,32,128]{2,1,0:T(8,128)(2,1)}, bf16[4,32,128]{2,1,0:T(8,128)(2,1)S(1)}, u32[]{:S(2)}, u32[]{:S(2)}) collective-permute-start(bf16[4,32,128]{2,1,0:T(8,128)(2,1)} %bitcast.11), channel_id=1, source_target_pairs={{0,12},{1,13},{2,14},{3,15},{4,8},{5,9},{6,10},{7,11},{8,4},{9,5},... | collective-permute-start | bytes 98312 | tf_op jit(solution)/shard_map/ppermute | solution.py:264
  5.1 5.0 %collective-permute-start.1 = (bf16[4,32,128]{2,1,0:T(8,128)(2,1)}, bf16[4,32,128]{2,1,0:T(8,128)(2,1)S(1)}, u32[]{:S(2)}, u32[]{:S(2)}) collective-permute-start(bf16[4,32,128]{2,1,0:T(8,128)(2,1)} %bitcast.12), channel_id=1, source_target_pairs={{0,8},{1,9},{2,10},{3,11},{4,12},{5,13},{6,14},{7,15},{8,0},{9,1},... | collective-permute-start | bytes 98312 | tf_op jit(solution)/shard_map/ppermute | solution.py:264
  5.1 4.1 %collective-permute-start = (bf16[4,32,128]{2,1,0:T(8,128)(2,1)}, bf16[4,32,128]{2,1,0:T(8,128)(2,1)S(1)}, u32[]{:S(2)}, u32[]{:S(2)}) collective-permute-start(bf16[4,32,128]{2,1,0:T(8,128)(2,1)} %bitcast.13), channel_id=1, source_target_pairs={{0,4},{1,5},{2,6},{3,7},{4,0},{5,1},{6,2},{7,3},{8,12},{9,13},{10,... | collective-permute-start | bytes 98312 | tf_op jit(solution)/shard_map/ppermute | solution.py:264
  10.2 4.3 %collective-permute-start.5 = (bf16[2,128,128]{2,1,0:T(8,128)(2,1)S(1)}, bf16[2,128,128]{2,1,0:T(8,128)(2,1)S(1)}, u32[]{:S(2)}, u32[]{:S(2)}) collective-permute-start(bf16[2,128,128]{2,1,0:T(8,128)(2,1)S(1)} %get-tuple-element.33), channel_id=1, source_target_pairs={{0,2},{1,3},{2,0},{3,1},{4,6},{5,7},{6,4},{7,5},{8,10},{9,11},{10,... | collective-permute-start | bytes 196616 | tf_op jit(solution)/shard_map/ppermute | solution.py:264
  11.7 6.4 %collective-permute-start.3 = (bf16[4,128,128]{2,1,0:T(8,128)(2,1)S(1)}, bf16[4,128,128]{2,1,0:T(8,128)(2,1)S(1)}, u32[]{:S(2)}, u32[]{:S(2)}) collective-permute-start(bf16[4,128,128]{2,1,0:T(8,128)(2,1)S(1)} %constant_dynamic-update-slice_fusion.refs_0_), channel_id=1, source_target_pairs={{0,1},{1,0},{2,3},{3,2},{4,5},{5,4},{6,7},{7,6},{8,9},{9,8},{10,11... | collective-permute-start | bytes 393224 | tf_op jit(solution)/shard_map/ppermute | solution.py:264
  11.7 4.5 %collective-permute-start.9 = (bf16[2,128,128]{2,1,0:T(8,128)(2,1)S(1)}, bf16[2,128,128]{2,1,0:T(8,128)(2,1)S(1)}, u32[]{:S(2)}, u32[]{:S(2)}) collective-permute-start(bf16[2,128,128]{2,1,0:T(8,128)(2,1)S(1)} %get-tuple-element.34), channel_id=1, source_target_pairs={{0,2},{1,3},{2,0},{3,1},{4,6},{5,7},{6,4},{7,5},{8,10},{9,11},{10,... | collective-permute-start | bytes 196616 | tf_op jit(solution)/shard_map/ppermute | solution.py:264
  14.5 1.8 %collective-permute-start.6 = (bf16[2,128,128]{2,1,0:T(8,128)(2,1)S(1)}, bf16[2,128,128]{2,1,0:T(8,128)(2,1)S(1)}, u32[]{:S(2)}, u32[]{:S(2)}) collective-permute-start(bf16[2,128,128]{2,1,0:T(8,128)(2,1)S(1)} %collective-permute-done.5.refs_0_), channel_id=1, source_target_pairs={{0,1},{1,0},{2,3},{3,2},{4,5},{5,4},{6,7},{7,6},{8,9},{9,8},{10,11... | collective-permute-start | bytes 196616 | tf_op jit(solution)/shard_map/ppermute | solution.py:264
  16.2 4.3 %collective-permute-start.10 = (bf16[2,128,128]{2,1,0:T(8,128)(2,1)S(1)}, bf16[2,128,128]{2,1,0:T(8,128)(2,1)S(1)}, u32[]{:S(2)}, u32[]{:S(2)}) collective-permute-start(bf16[2,128,128]{2,1,0:T(8,128)(2,1)S(1)} %collective-permute-done.9.refs_0_), channel_id=1, source_target_pairs={{0,1},{1,0},{2,3},{3,2},{4,5},{5,4},{6,7},{7,6},{8,9},{9,8},{10,11... | collective-permute-start | bytes 196616 | tf_op jit(solution)/shard_map/ppermute | solution.py:264
  17.6 4.9 %collective-permute-start.7 = (bf16[2,136,128]{2,1,0:T(8,128)(2,1)S(1)}, bf16[2,136,128]{2,1,0:T(8,128)(2,1)S(1)}, u32[]{:S(2)}, u32[]{:S(2)}) collective-permute-start(bf16[2,136,128]{2,1,0:T(8,128)(2,1)S(1)} %get-tuple-element.26), channel_id=1, source_target_pairs={{0,1},{1,0},{2,3},{3,2},{4,5},{5,4},{6,7},{7,6},{8,9},{9,8},{10,11... | collective-permute-start | bytes 208904 | tf_op jit(solution)/shard_map/ppermute | solution.py:264
  20.4 4.5 %collective-permute-start.4 = (bf16[4,136,128]{2,1,0:T(8,128)(2,1)S(1)}, bf16[4,136,128]{2,1,0:T(8,128)(2,1)S(1)}, u32[]{:S(2)}, u32[]{:S(2)}) collective-permute-start(bf16[4,136,128]{2,1,0:T(8,128)(2,1)S(1)} %get-tuple-element.24), channel_id=1, source_target_pairs={{0,1},{1,0},{2,3},{3,2},{4,5},{5,4},{6,7},{7,6},{8,9},{9,8},{10,11... | collective-permute-start | bytes 417800 | tf_op jit(solution)/shard_map/ppermute | solution.py:264
  21.9 2.0 %collective-permute-start.11 = (bf16[2,136,128]{2,1,0:T(8,128)(2,1)S(1)}, bf16[2,136,128]{2,1,0:T(8,128)(2,1)S(1)}, u32[]{:S(2)}, u32[]{:S(2)}) collective-permute-start(bf16[2,136,128]{2,1,0:T(8,128)(2,1)S(1)} %get-tuple-element.28), channel_id=1, source_target_pairs={{0,1},{1,0},{2,3},{3,2},{4,5},{5,4},{6,7},{7,6},{8,9},{9,8},{10,11... | collective-permute-start | bytes 208904 | tf_op jit(solution)/shard_map/ppermute | solution.py:264
  22.5 4.6 %collective-permute-start.8 = (bf16[2,136,128]{2,1,0:T(8,128)(2,1)S(1)}, bf16[2,136,128]{2,1,0:T(8,128)(2,1)S(1)}, u32[]{:S(2)}, u32[]{:S(2)}) collective-permute-start(bf16[2,136,128]{2,1,0:T(8,128)(2,1)S(1)} %shard_map.59), channel_id=1, source_target_pairs={{0,2},{1,3},{2,0},{3,1},{4,6},{5,7},{6,4},{7,5},{8,10},{9,11},{10,... | collective-permute-start | bytes 208904 | tf_op jit(solution)/shard_map/ppermute | solution.py:264
  23.9 4.4 %collective-permute-start.12 = (bf16[2,136,128]{2,1,0:T(8,128)(2,1)S(1)}, bf16[2,136,128]{2,1,0:T(8,128)(2,1)S(1)}, u32[]{:S(2)}, u32[]{:S(2)}) collective-permute-start(bf16[2,136,128]{2,1,0:T(8,128)(2,1)S(1)} %shard_map.61), channel_id=1, source_target_pairs={{0,2},{1,3},{2,0},{3,1},{4,6},{5,7},{6,4},{7,5},{8,10},{9,11},{10,... | collective-permute-start | bytes 208904 | tf_op jit(solution)/shard_map/ppermute | solution.py:264
  28.6 4.5 %collective-permute-start.13 = (bf16[136,128]{1,0:T(8,128)(2,1)S(1)}, bf16[136,128]{1,0:T(8,128)(2,1)S(1)}, u32[]{:S(2)}, u32[]{:S(2)}) collective-permute-start(bf16[136,128]{1,0:T(8,128)(2,1)S(1)} %get-tuple-element.30), channel_id=1, source_target_pairs={{0,4},{1,5},{2,6},{3,7},{4,0},{5,1},{6,2},{7,3},{8,12},{9,13},{10,... | collective-permute-start | bytes 104456 | tf_op jit(solution)/shard_map/ppermute | solution.py:264
  28.7 4.9 %collective-permute-start.14 = (bf16[136,128]{1,0:T(8,128)(2,1)S(1)}, bf16[136,128]{1,0:T(8,128)(2,1)S(1)}, u32[]{:S(2)}, u32[]{:S(2)}) collective-permute-start(bf16[136,128]{1,0:T(8,128)(2,1)S(1)} %get-tuple-element.31), channel_id=1, source_target_pairs={{0,8},{1,9},{2,10},{3,11},{4,12},{5,13},{6,14},{7,15},{8,0},{9,1},... | collective-permute-start | bytes 104456 | tf_op jit(solution)/shard_map/ppermute | solution.py:264
  30.8 5.7 %collective-permute-start.15 = (bf16[136,128]{1,0:T(8,128)(2,1)S(1)}, bf16[136,128]{1,0:T(8,128)(2,1)S(1)}, u32[]{:S(2)}, u32[]{:S(2)}) collective-permute-start(bf16[136,128]{1,0:T(8,128)(2,1)S(1)} %get-tuple-element.32), channel_id=1, source_target_pairs={{0,12},{1,13},{2,14},{3,15},{4,8},{5,9},{6,10},{7,11},{8,4},{9,5},... | collective-permute-start | bytes 104456 | tf_op jit(solution)/shard_map/ppermute | solution.py:264

commit v4 on v3

--- a/solution.py
+++ b/solution.py
@@ -12,7 +12,9 @@
 HEAD_DIM = 128
 LOW = -1e30
 STAT_ROWS = 8
-PARTS = 5
+PARTS = 2
+CHAINS = 16
+FAR_PARTS = 2
 
 VMEM = pl.BlockSpec(memory_space=pltpu.VMEM)
 HBM = pl.BlockSpec(memory_space=pltpu.HBM)
@@ -25,7 +27,8 @@
     unit = 4
     wide = []
     while unit < shards:
-        wide.append([unit, 2 * unit, 3 * unit])
+        one, two = unit, 2 * unit + 1
+        wide.append([one, two, one ^ two])
         unit *= 4
     return masks + wide[::-1]
 
@@ -73,7 +76,7 @@
     return num, peak, total
 
 
-def prep_kernel(info_ref, len_hbm, off_hbm, q_hbm, k_hbm, v_hbm, q_ref, k_ref, vt_ref, mask_ref, v_ref, len_ref, off_ref, sem):
+def prep_kernel(local_rows, origins, info_ref, len_hbm, off_hbm, q_hbm, k_hbm, v_hbm, q_ref, k_ref, vt_ref, mask_ref, near_ref, far_ref, v_ref, len_ref, off_ref, sem):
     micros, key_count, rows = mask_ref.shape
     chunk = key_count // PARTS
 
@@ -108,6 +111,16 @@
         mask_ref[micro] = jnp.where(key <= last, 0.0, LOW).astype(mask_ref.dtype)
         for head in range(KV_HEADS):
             vt_ref[micro * KV_HEADS + head, HEAD_DIM:] = jnp.ones((STAT_ROWS, key_count), vt_ref.dtype)
+    for chosen_ref, masks in zip((near_ref, far_ref), origins):
+        shape = chosen_ref.shape
+        lane = lax.broadcasted_iota(jnp.int32, (shape[0], 1), 0)
+        width = shape[0] // len(masks)
+        origin = jnp.full((shape[0], 1), masks[0], jnp.int32)
+        for index, mask in enumerate(masks):
+            origin = jnp.where(lane // width == index, mask, origin)
+        place = (origin ^ info_ref[0]) * local_rows + lane % local_rows
+        same = place == lax.broadcasted_iota(jnp.int32, shape, 1)
+        chosen_ref[...] = same.astype(jnp.float32).astype(chosen_ref.dtype)
     for micro in range(micros):
         for part in range(PARTS):
             cut = slice(part * chunk, (part + 1) * chunk)
@@ -119,23 +132,13 @@
         copy.wait()
 
 
-def attend_kernel(local_rows, masks, sends, base, info_ref, *refs):
+def attend_kernel(sends, base, info_ref, *refs):
     count = len(sends)
-    q_refs, (k_ref, vt_ref, mask_ref), refs = refs[:count], refs[count : count + 3], refs[count + 3 :]
-    out_refs, s_ref = refs[:count], refs[count]
-    groups = q_refs[0].shape[0]
-    block = q_refs[0].shape[1]
+    q_refs, refs = refs[:count], refs[count:]
+    k_ref, vt_ref, mask_ref, chosen_ref, *refs = refs
+    out_refs, (s_ref, top_ref) = refs[:count], refs[count:]
+    groups, block = out_refs[0].shape[0], q_refs[0].shape[1]
     lanes = block * count
-    table = mask_ref.shape[2]
-    me = info_ref[0]
-    width = lanes // len(masks)
-    lane = lax.broadcasted_iota(jnp.int32, (lanes, table), 0)
-    origin = jnp.full((lanes, table), masks[0], jnp.int32)
-    for index, mask in enumerate(masks):
-        origin = jnp.where(lane // width == index, mask, origin)
-    row = (origin ^ me) * local_rows + lane % local_rows
-    chosen = (row == lax.broadcasted_iota(jnp.int32, (lanes, table), 1)).astype(jnp.float32)
-    chosen = chosen.astype(k_ref.dtype)
     unit = math.log2(math.e) / math.sqrt(HEAD_DIM)
 
     def score(group):
@@ -144,18 +147,21 @@
         rows = jnp.concatenate([ref[group] for ref in q_refs], axis=0)
         scores = lax.dot_general(
             jnp.concatenate([k_ref[micro, :, span], mask_ref[micro]], axis=1),
-            jnp.concatenate([rows, chosen], axis=1),
+            jnp.concatenate([rows, chosen_ref[...]], axis=1),
             (((1,), (1,)), ((), ())),
             preferred_element_type=jnp.float32,
         )
         s_ref[group % 2] = scores
-        return jnp.max(scores, axis=0, keepdims=True)
-
-    def weigh(group, top):
+        top_ref[group % 2] = jnp.max(scores.reshape(-1, CHAINS, lanes), axis=0)
+
+    def weigh(group):
+        top = jnp.max(top_ref[group % 2], axis=0, keepdims=True)
         some = top > LOW / 2
         top = jnp.where(some, top, 0.0)
         weights = jnp.exp2((s_ref[group % 2] - top) * unit)
-        num = jnp.dot(vt_ref[base + group], weights.astype(vt_ref.dtype), preferred_element_type=jnp.float32)
+        num = jnp.dot(
+            vt_ref[base + group], weights.astype(vt_ref.dtype), preferred_element_type=jnp.float32
+        )
         total = num[HEAD_DIM : HEAD_DIM + 1]
         peak = jnp.where(some, top * unit, LOW)
         for index, send in enumerate(sends):
@@ -163,11 +169,14 @@
             part = (num[:HEAD_DIM, cut], peak[:, cut], total[:, cut])
             out_refs[index][group] = packed(*part) if send else kept(*part)
 
-    top = score(0)
+    score(0)
     for group in range(groups):
-        following = score(group + 1) if group + 1 < groups else None
-        weigh(group, top)
-        top = following
+
+        @pl.when(info_ref[0] >= 0)
+        def _(group=group):
+            if group + 1 < groups:
+                score(group + 1)
+            weigh(group)
 
 
 def merge_kernel(ways, received, keep_ref, *refs):
@@ -255,6 +264,7 @@
     shards = lax.axis_size("blk")
     key_count = keys.shape[1]
     masks = digit_masks(shards)
+    beyond = masks[1][0]
     stacked = HEAD_DIM + STAT_ROWS
     table = -(-shards * local_rows // HEAD_DIM) * HEAD_DIM
     info = jnp.reshape(lax.axis_index("blk"), (1,)).astype(jnp.int32)
@@ -265,60 +275,68 @@
 
     own = queries.reshape(micro_count, local_rows, KV_HEADS, share, HEAD_DIM)
     own = own.transpose(0, 2, 3, 1, 4).reshape(groups, width, HEAD_DIM)
-    near, keys_in, values_t, seen = call(
-        prep_kernel,
+    origin = [0]
+    for level in masks[:1:-1]:
+        origin = [base ^ mask for mask in [0] + level for base in origin]
+    block = len(origin) * width
+    near_origin, far_origin = ([base ^ shift for shift in shifts for base in origin] for shifts in ((0, 1), (beyond, beyond ^ 1)))
+    near, keys_in, values_t, seen, near_rows, far_rows = call(
+        functools.partial(prep_kernel, local_rows, (near_origin, far_origin)),
         [
             struct(own.shape, low),
             struct(keys.shape, low),
             struct((groups, stacked, key_count), low),
             struct((micro_count, key_count, table), low),
+            struct((2 * block, table), low),
+            struct((2 * block, table), low),
         ],
         [SMEM] + [HBM] * 5,
         nbytes=2 * keys.size * 2,
         grant=8,
-        scratch=[pltpu.VMEM(values.shape, low), pltpu.SMEM(lengths.shape, jnp.int32), pltpu.SMEM(offsets.shape, jnp.int32), pltpu.SemaphoreType.DMA((2 * micro_count * PARTS + 3,))],
+        scratch=[
+            pltpu.VMEM(values.shape, low),
+            pltpu.SMEM(lengths.shape, jnp.int32),
+            pltpu.SMEM(offsets.shape, jnp.int32),
+            pltpu.SemaphoreType.DMA((2 * micro_count * PARTS + 3,)),
+        ],
     )(info, *[in_hbm(part) for part in (lengths, offsets, own, keys, values)])
 
-    origin = [0]
     source = own
     for level in masks[:1:-1]:
         got = [swap(source, mask) for mask in level]
         near = source = jnp.concatenate([near] + got, axis=1)
-        origin = [base ^ mask for mask in [0] + level for base in origin]
     block = near.shape[1]
 
-    def attend(rows, shifts, sends, base=0):
-        count, held = len(rows), rows[0].shape[0]
+    def attend(rows, chosen, cut):
+        count, held = len(rows), cut[1] - cut[0]
         return call(
-            functools.partial(
-                attend_kernel,
-                local_rows,
-                [mask ^ shift for shift in shifts for mask in origin],
-                sends,
-                base,
-            ),
-            [struct((held, stacked, block), low if send else jnp.float32) for send in sends],
-            [SMEM] + [VMEM] * (count + 3),
+            functools.partial(attend_kernel, [False, True], cut[0]),
+            [struct((held, stacked, block), part) for part in (jnp.float32, low)],
+            [SMEM] + [VMEM] * (count + 4),
             flops=6 * held * block * count * key_count * HEAD_DIM,
             grant=16,
-            scratch=[pltpu.VMEM((2, key_count, block * count), jnp.float32)],
-        )(info, *rows, keys_in, values_t, seen)
+            scratch=[
+                pltpu.VMEM((2, key_count, block * count), jnp.float32),
+                pltpu.VMEM((2, CHAINS, block * count), jnp.float32),
+            ],
+        )(info, *rows, keys_in, values_t, seen, chosen)
 
     def join(send, keep, got):
         outs = struct(keep.shape, low if send else jnp.float32)
         return call(functools.partial(join_kernel, send), outs, [VMEM] * 2)(keep, got)
 
-    micros = range(micro_count)
+    held = groups // FAR_PARTS
+    cuts = [(p * held, (p + 1) * held) for p in range(FAR_PARTS)]
     near_across = swap(near, 1)
-    fars = [swap(near[m * KV_HEADS : (m + 1) * KV_HEADS], 2) for m in micros]
-    near_keep, near_send = attend([near, near_across], [0, 1], [False, True])
+    fars = [swap(near[slice(*cut)], beyond) for cut in cuts]
+    near_keep, near_send = attend([near, near_across], near_rows, (0, groups))
     near_got = swap(near_send, 1)
     got = []
-    for m in micros:
-        across = swap(fars[m], 1)
-        far_keep, far_send = attend([fars[m], across], [2, 3], [False, True], m * KV_HEADS)
-        far_got = swap(far_send, 1)
-        got.append(swap(join(True, far_keep, far_got), 2))
+    for p, cut in enumerate(cuts):
+        across = swap(fars[p], 1)
+        keep, send = attend([fars[p], across], far_rows, cut)
+        keep = join(True, keep, swap(send, 1))
+        got.append(swap(keep, beyond))
     got = [jnp.concatenate(got, axis=0)]
     keep = join(False, near_keep, near_got)
     lanes = block

time: 37.4 us -> 36 us (0.963)
  the two profiles are of different devices: /device:TPU:0 before, /device:TPU:1 now
where the time goes in v4:
time: 36 us; the launch traced here: 35.8 us
  starting transfers between devices  17.1 us (48%)
  waiting for transfers between devices  11.1 us (31%)
  Pallas kernels  7.53 us (21%)
    ppermute x16, starting transfers between devices, swap(): return lax.ppermute(part, 'blk', pairs(shards, mask))  17.1 us
    ppermute x16, waiting for transfers between devices, swap(): return lax.ppermute(part, 'blk', pairs(shards, mask))  11.1 us
    pallas_call x3, Pallas kernels, attend(): call(functools.partial(attend_kernel, [False, True], cut[0]), [struct((he...  4.64 us
    pallas_call x1, Pallas kernels, program(): call(functools.partial(prep_kernel, local_rows, (near_origin, far_origin)...  1.78 us
    pallas_call x1, Pallas kernels, program(): call(final_kernel, struct((groups * width, HEAD_DIM), low), [VMEM] * (1 +...  0.75 us
  transfers between devices with their start and end apart: 16, of which 8 were waited for; matrix products, arithmetic and copies ran while one was open for 0% of the time, Pallas kernels for 18%

profile of v4, /device:TPU:1, one launch (start us, length us, event | category | flops | bytes accessed | tf_op | source)
XLA Modules:
  0.0 35.8 jit_solution(18399839195849832641)
XLA Ops:
  0.0 4.7 %collective-permute-start.2 = (bf16[4,32,128]{2,1,0:T(8,128)(2,1)}, bf16[4,32,128]{2,1,0:T(8,128)(2,1)S(1)}, u32[]{:S(2)}, u32[]{:S(2)}) collective-permute-start(bf16[4,32,128]{2,1,0:T(8,128)(2,1)} %bitcast.11), channel_id=1, source_target_pairs={{0,13},{1,12},{2,15},{3,14},{4,9},{5,8},{6,11},{7,10},{8,5},{9,4},... | collective-permute-start | bytes 98312 | tf_op jit(solution)/shard_map/ppermute | solution.py:274
  4.7 0.0 collective-permute-start.1
  4.7 0.3 collective-permute-start
  5.0 1.8 %shard_map.55 = (bf16[4,32,128]{2,1,0:T(8,128)(2,1)S(1)}, bf16[2,1280,256]{2,1,0:T(8,128)(2,1)S(1)}, bf16[4,136,1280]{2,1,0:T(8,128)(2,1)S(1)}, bf16[2,1280,128]...) custom-call(s32[1]{0:T(128)} %bitcast.info_ref, s32[2]{0:T(128)} %len_hbm.1, ...), custom_call_target="tpu_custom_call" | custom-call | bytes 2621440 | tf_op jit(solution)/shard_map/pallas_call | solution.py:283
  6.8 1.2 %collective-permute-done = bf16[4,32,128]{2,1,0:T(8,128)(2,1)S(1)} collective-permute-done((bf16[4,32,128]{2,1,0:T(8,128)(2,1)}, bf16[4,32,128]{2,1,0:T(8,128)(2,1)S(1)}, u32[]{:S(2)}, u32[]{:S(2)}) %collective-permute-start) | collective-permute-done | bytes 32800 | tf_op jit(solution)/shard_map/ppermute | solution.py:274
  8.0 1.1 %collective-permute-done.1 = bf16[4,32,128]{2,1,0:T(8,128)(2,1)S(1)} collective-permute-done((bf16[4,32,128]{2,1,0:T(8,128)(2,1)}, bf16[4,32,128]{2,1,0:T(8,128)(2,1)S(1)}, u32[]{:S(2)}, u32[]{:S(2)}) %collective-permute-start.1) | collective-permute-done | bytes 32800 | tf_op jit(solution)/shard_map/ppermute | solution.py:274
  9.2 0.0 collective-permute-done.2
  9.2 1.3 %collective-permute-start.5 = (bf16[2,128,128]{2,1,0:T(8,128)(2,1)S(1)}, bf16[2,128,128]{2,1,0:T(8,128)(2,1)S(1)}, u32[]{:S(2)}, u32[]{:S(2)}) collective-permute-start(bf16[2,128,128]{2,1,0:T(8,128)(2,1)S(1)} %get-tuple-element.37), channel_id=1, source_target_pairs={{0,2},{1,3},{2,0},{3,1},{4,6},{5,7},{6,4},{7,5},{8,10},{9,11},{10,... | collective-permute-start | bytes 196616 | tf_op jit(solution)/shard_map/ppermute | solution.py:274
  10.5 0.3 collective-permute-start.3
  10.8 0.2 collective-permute-start.9
  11.0 1.8 %collective-permute-done.5.refs_0_ = bf16[2,128,128]{2,1,0:T(8,128)(2,1)S(1)} collective-permute-done((bf16[2,128,128]{2,1,0:T(8,128)(2,1)S(1)}, bf16[2,128,128]{2,1,0:T(8,128)(2,1)S(1)}, u32[]{:S(2)}, u32[]{:S(2)}) %collective-permute-start.5) | collective-permute-done | bytes 65568 | tf_op jit(solution)/shard_map/ppermute | solution.py:274
  12.9 0.9 %collective-permute-start.6 = (bf16[2,128,128]{2,1,0:T(8,128)(2,1)S(1)}, bf16[2,128,128]{2,1,0:T(8,128)(2,1)S(1)}, u32[]{:S(2)}, u32[]{:S(2)}) collective-permute-start(bf16[2,128,128]{2,1,0:T(8,128)(2,1)S(1)} %collective-permute-done.5.refs_0_), channel_id=1, source_target_pairs={{0,1},{1,0},{2,3},{3,2},{4,5},{5,4},{6,7},{7,6},{8,9},{9,8},{10,11... | collective-permute-start | bytes 196616 | tf_op jit(solution)/shard_map/ppermute | solution.py:274
  13.8 0.5 %collective-permute-done.9.refs_0_ = bf16[2,128,128]{2,1,0:T(8,128)(2,1)S(1)} collective-permute-done((bf16[2,128,128]{2,1,0:T(8,128)(2,1)S(1)}, bf16[2,128,128]{2,1,0:T(8,128)(2,1)S(1)}, u32[]{:S(2)}, u32[]{:S(2)}) %collective-permute-start.9) | collective-permute-done | bytes 65568 | tf_op jit(solution)/shard_map/ppermute | solution.py:274
  14.3 1.1 %collective-permute-start.10 = (bf16[2,128,128]{2,1,0:T(8,128)(2,1)S(1)}, bf16[2,128,128]{2,1,0:T(8,128)(2,1)S(1)}, u32[]{:S(2)}, u32[]{:S(2)}) collective-permute-start(bf16[2,128,128]{2,1,0:T(8,128)(2,1)S(1)} %collective-permute-done.9.refs_0_), channel_id=1, source_target_pairs={{0,1},{1,0},{2,3},{3,2},{4,5},{5,4},{6,7},{7,6},{8,9},{9,8},{10,11... | collective-permute-start | bytes 196616 | tf_op jit(solution)/shard_map/ppermute | solution.py:274
  15.3 0.0 collective-permute-done.6.refs_1_
  15.3 1.2 %shard_map.58 = (f32[2,136,128]{2,1,0:T(8,128)S(1)}, bf16[2,136,128]{2,1,0:T(8,128)(2,1)S(1)}) custom-call(s32[1]{0:T(128)} %bitcast.info_ref, bf16[2,128,128]{2,1,0:T(8,128)(2,1)S(1)} %collective-permute-done.5.refs_0_, bf16[2,128,128]{2,1,0:T(8,128)(2,1)S(1)} %collective-permute-done.6.refs_1_, bf16[2,1280,256]{2,1,0:T(8,128)(2,1)S(1)} %get-tuple-element.22.refs_2_, ...), custom_call_target="tpu_custom_call" | custom-call | flops 503316480 | tf_op jit(solution)/shard_map/pallas_call | solution.py:312
  16.6 0.1 collective-permute-start.7
  16.6 0.0 collective-permute-done.3.refs_1_
  16.6 2.2 %shard_map.56 = (f32[4,136,128]{2,1,0:T(8,128)S(1)}, bf16[4,136,128]{2,1,0:T(8,128)(2,1)S(1)}) custom-call(s32[1]{0:T(128)} %bitcast.info_ref, bf16[4,128,128]{2,1,0:T(8,128)(2,1)S(1)} %constant_dynamic-update-slice_fusion.refs_0_, bf16[4,128,128]{2,1,0:T(8,128)(2,1)S(1)} %collective-permute-done.3.refs_1_, ...), custom_call_target="tpu_custom_call" | custom-call | flops 1006632960 | tf_op jit(solution)/shard_map/pallas_call | solution.py:312
  18.8 0.5 %collective-permute-start.4 = (bf16[4,136,128]{2,1,0:T(8,128)(2,1)S(1)}, bf16[4,136,128]{2,1,0:T(8,128)(2,1)S(1)}, u32[]{:S(2)}, u32[]{:S(2)}) collective-permute-start(bf16[4,136,128]{2,1,0:T(8,128)(2,1)S(1)} %get-tuple-element.27), channel_id=1, source_target_pairs={{0,1},{1,0},{2,3},{3,2},{4,5},{5,4},{6,7},{7,6},{8,9},{9,8},{10,11... | collective-permute-start | bytes 417800 | tf_op jit(solution)/shard_map/ppermute | solution.py:274
  19.4 0.0 collective-permute-done.10.refs_1_
  19.4 1.2 %shard_map.60 = (f32[2,136,128]{2,1,0:T(8,128)S(1)}, bf16[2,136,128]{2,1,0:T(8,128)(2,1)S(1)}) custom-call(s32[1]{0:T(128)} %bitcast.info_ref, bf16[2,128,128]{2,1,0:T(8,128)(2,1)S(1)} %collective-permute-done.9.refs_0_, bf16[2,128,128]{2,1,0:T(8,128)(2,1)S(1)} %collective-permute-done.10.refs_1_, bf16[2,1280,256]{2,1,0:T(8,128)(2,1)S(1)} %get-tuple-element.22.refs_2_, ...), custom_call_target="tpu_custom_call" | custom-call | flops 503316480 | tf_op jit(solution)/shard_map/pallas_call | solution.py:312
  20.6 0.1 collective-permute-start.11
  20.7 0.0 collective-permute-done.7.got_ref
  20.8 1.4 %collective-permute-start.8 = (bf16[2,136,128]{2,1,0:T(8,128)(2,1)S(1)}, bf16[2,136,128]{2,1,0:T(8,128)(2,1)S(1)}, u32[]{:S(2)}, u32[]{:S(2)}) collective-permute-start(bf16[2,136,128]{2,1,0:T(8,128)(2,1)S(1)} %shard_map.59), channel_id=1, source_target_pairs={{0,2},{1,3},{2,0},{3,1},{4,6},{5,7},{6,4},{7,5},{8,10},{9,11},{10,... | collective-permute-start | bytes 208904 | tf_op jit(solution)/shard_map/ppermute | solution.py:274
  22.2 0.0 collective-permute-done.11.got_ref
  22.3 0.9 %collective-permute-start.12 = (bf16[2,136,128]{2,1,0:T(8,128)(2,1)S(1)}, bf16[2,136,128]{2,1,0:T(8,128)(2,1)S(1)}, u32[]{:S(2)}, u32[]{:S(2)}) collective-permute-start(bf16[2,136,128]{2,1,0:T(8,128)(2,1)S(1)} %shard_map.61), channel_id=1, source_target_pairs={{0,2},{1,3},{2,0},{3,1},{4,6},{5,7},{6,4},{7,5},{8,10},{9,11},{10,... | collective-permute-start | bytes 208904 | tf_op jit(solution)/shard_map/ppermute | solution.py:274
  23.1 0.0 collective-permute-done.4.got_ref
  23.1 0.1 shard_map.57.keep_ref
  23.2 0.8 %collective-permute-done.8 = bf16[2,136,128]{2,1,0:T(8,128)(2,1)S(1)} collective-permute-done((bf16[2,136,128]{2,1,0:T(8,128)(2,1)S(1)}, bf16[2,136,128]{2,1,0:T(8,128)(2,1)S(1)}, u32[]{:S(2)}, u32[]{:S(2)}) %collective-permute-start.8) | collective-permute-done | bytes 69664 | tf_op jit(solution)/shard_map/ppermute | solution.py:274
  24.0 1.7 %collective-permute-done.12 = bf16[2,136,128]{2,1,0:T(8,128)(2,1)S(1)} collective-permute-done((bf16[2,136,128]{2,1,0:T(8,128)(2,1)S(1)}, bf16[2,136,128]{2,1,0:T(8,128)(2,1)S(1)}, u32[]{:S(2)}, u32[]{:S(2)}) %collective-permute-start.12) | collective-permute-done | bytes 69664 | tf_op jit(solution)/shard_map/ppermute | solution.py:274
  25.7 0.2 shard_map.62
  25.9 1.4 %collective-permute-start.13 = (bf16[136,128]{1,0:T(8,128)(2,1)S(1)}, bf16[136,128]{1,0:T(8,128)(2,1)S(1)}, u32[]{:S(2)}, u32[]{:S(2)}) collective-permute-start(bf16[136,128]{1,0:T(8,128)(2,1)S(1)} %get-tuple-element.34), channel_id=1, source_target_pairs={{0,4},{1,5},{2,6},{3,7},{4,0},{5,1},{6,2},{7,3},{8,12},{9,13},{10,... | collective-permute-start | bytes 104456 | tf_op jit(solution)/shard_map/ppermute | solution.py:274
  27.3 2.6 %collective-permute-start.14 = (bf16[136,128]{1,0:T(8,128)(2,1)S(1)}, bf16[136,128]{1,0:T(8,128)(2,1)S(1)}, u32[]{:S(2)}, u32[]{:S(2)}) collective-permute-start(bf16[136,128]{1,0:T(8,128)(2,1)S(1)} %get-tuple-element.35), channel_id=1, source_target_pairs={{0,9},{1,8},{2,11},{3,10},{4,13},{5,12},{6,15},{7,14},{8,1},{9,0},... | collective-permute-start | bytes 104456 | tf_op jit(solution)/shard_map/ppermute | solution.py:274
  29.9 1.3 %collective-permute-start.15 = (bf16[136,128]{1,0:T(8,128)(2,1)S(1)}, bf16[136,128]{1,0:T(8,128)(2,1)S(1)}, u32[]{:S(2)}, u32[]{:S(2)}) collective-permute-start(bf16[136,128]{1,0:T(8,128)(2,1)S(1)} %get-tuple-element.36), channel_id=1, source_target_pairs={{0,13},{1,12},{2,15},{3,14},{4,9},{5,8},{6,11},{7,10},{8,5},{9,4},... | collective-permute-start | bytes 104456 | tf_op jit(solution)/shard_map/ppermute | solution.py:274
  31.2 0.0 collective-permute-done.13.refs_0_
  31.2 0.4 %collective-permute-done.14.refs_1_ = bf16[136,128]{1,0:T(8,128)(2,1)S(1)} collective-permute-done((bf16[136,128]{1,0:T(8,128)(2,1)S(1)}, bf16[136,128]{1,0:T(8,128)(2,1)S(1)}, u32[]{:S(2)}, u32[]{:S(2)}) %collective-permute-start.14) | collective-permute-done | bytes 34848 | tf_op jit(solution)/shard_map/ppermute | solution.py:274
  31.6 3.5 %collective-permute-done.15.refs_2_ = bf16[136,128]{1,0:T(8,128)(2,1)S(1)} collective-permute-done((bf16[136,128]{1,0:T(8,128)(2,1)S(1)}, bf16[136,128]{1,0:T(8,128)(2,1)S(1)}, u32[]{:S(2)}, u32[]{:S(2)}) %collective-permute-start.15) | collective-permute-done | bytes 34848 | tf_op jit(solution)/shard_map/ppermute | solution.py:274
  35.1 0.7 %shard_map.63 = bf16[128,128]{1,0:T(8,128)(2,1)} custom-call(f32[136,128]{1,0:T(8,128)S(1)} %get-tuple-element.33.keep_ref, bf16[136,128]{1,0:T(8,128)(2,1)S(1)} %collective-permute-done.13.refs_0_, bf16[136,128]{1,0:T(8,128)(2,1)S(1)} %collective-permute-done.14.refs_1_, bf16[136,128]{1,0:T(8,128)(2,1)S(1)} %collective-permute-done.15.refs_2_), custom_call_target="tpu_custom_call" | custom-call | tf_op jit(solution)/shard_map/pallas_call | solution.py:358
  (8 shorter events, 0.2 us)
Async XLA Ops:
  0.0 9.2 %collective-permute-start.2 = (bf16[4,32,128]{2,1,0:T(8,128)(2,1)}, bf16[4,32,128]{2,1,0:T(8,128)(2,1)S(1)}, u32[]{:S(2)}, u32[]{:S(2)}) collective-permute-start(bf16[4,32,128]{2,1,0:T(8,128)(2,1)} %bitcast.11), channel_id=1, source_target_pairs={{0,13},{1,12},{2,15},{3,14},{4,9},{5,8},{6,11},{7,10},{8,5},{9,4},... | collective-permute-start | bytes 98312 | tf_op jit(solution)/shard_map/ppermute | solution.py:274
  4.7 4.4 %collective-permute-start.1 = (bf16[4,32,128]{2,1,0:T(8,128)(2,1)}, bf16[4,32,128]{2,1,0:T(8,128)(2,1)S(1)}, u32[]{:S(2)}, u32[]{:S(2)}) collective-permute-start(bf16[4,32,128]{2,1,0:T(8,128)(2,1)} %bitcast.12), channel_id=1, source_target_pairs={{0,9},{1,8},{2,11},{3,10},{4,13},{5,12},{6,15},{7,14},{8,1},{9,0},... | collective-permute-start | bytes 98312 | tf_op jit(solution)/shard_map/ppermute | solution.py:274
  4.7 3.3 %collective-permute-start = (bf16[4,32,128]{2,1,0:T(8,128)(2,1)}, bf16[4,32,128]{2,1,0:T(8,128)(2,1)S(1)}, u32[]{:S(2)}, u32[]{:S(2)}) collective-permute-start(bf16[4,32,128]{2,1,0:T(8,128)(2,1)} %bitcast.13), channel_id=1, source_target_pairs={{0,4},{1,5},{2,6},{3,7},{4,0},{5,1},{6,2},{7,3},{8,12},{9,13},{10,... | collective-permute-start | bytes 98312 | tf_op jit(solution)/shard_map/ppermute | solution.py:274
  9.2 3.7 %collective-permute-start.5 = (bf16[2,128,128]{2,1,0:T(8,128)(2,1)S(1)}, bf16[2,128,128]{2,1,0:T(8,128)(2,1)S(1)}, u32[]{:S(2)}, u32[]{:S(2)}) collective-permute-start(bf16[2,128,128]{2,1,0:T(8,128)(2,1)S(1)} %get-tuple-element.37), channel_id=1, source_target_pairs={{0,2},{1,3},{2,0},{3,1},{4,6},{5,7},{6,4},{7,5},{8,10},{9,11},{10,... | collective-permute-start | bytes 196616 | tf_op jit(solution)/shard_map/ppermute | solution.py:274
  10.5 6.1 %collective-permute-start.3 = (bf16[4,128,128]{2,1,0:T(8,128)(2,1)S(1)}, bf16[4,128,128]{2,1,0:T(8,128)(2,1)S(1)}, u32[]{:S(2)}, u32[]{:S(2)}) collective-permute-start(bf16[4,128,128]{2,1,0:T(8,128)(2,1)S(1)} %constant_dynamic-update-slice_fusion.refs_0_), channel_id=1, source_target_pairs={{0,1},{1,0},{2,3},{3,2},{4,5},{5,4},{6,7},{7,6},{8,9},{9,8},{10,11... | collective-permute-start | bytes 393224 | tf_op jit(solution)/shard_map/ppermute | solution.py:274
  10.8 3.4 %collective-permute-start.9 = (bf16[2,128,128]{2,1,0:T(8,128)(2,1)S(1)}, bf16[2,128,128]{2,1,0:T(8,128)(2,1)S(1)}, u32[]{:S(2)}, u32[]{:S(2)}) collective-permute-start(bf16[2,128,128]{2,1,0:T(8,128)(2,1)S(1)} %get-tuple-element.38), channel_id=1, source_target_pairs={{0,2},{1,3},{2,0},{3,1},{4,6},{5,7},{6,4},{7,5},{8,10},{9,11},{10,... | collective-permute-start | bytes 196616 | tf_op jit(solution)/shard_map/ppermute | solution.py:274
  12.9 2.4 %collective-permute-start.6 = (bf16[2,128,128]{2,1,0:T(8,128)(2,1)S(1)}, bf16[2,128,128]{2,1,0:T(8,128)(2,1)S(1)}, u32[]{:S(2)}, u32[]{:S(2)}) collective-permute-start(bf16[2,128,128]{2,1,0:T(8,128)(2,1)S(1)} %collective-permute-done.5.refs_0_), channel_id=1, source_target_pairs={{0,1},{1,0},{2,3},{3,2},{4,5},{5,4},{6,7},{7,6},{8,9},{9,8},{10,11... | collective-permute-start | bytes 196616 | tf_op jit(solution)/shard_map/ppermute | solution.py:274
  14.3 5.1 %collective-permute-start.10 = (bf16[2,128,128]{2,1,0:T(8,128)(2,1)S(1)}, bf16[2,128,128]{2,1,0:T(8,128)(2,1)S(1)}, u32[]{:S(2)}, u32[]{:S(2)}) collective-permute-start(bf16[2,128,128]{2,1,0:T(8,128)(2,1)S(1)} %collective-permute-done.9.refs_0_), channel_id=1, source_target_pairs={{0,1},{1,0},{2,3},{3,2},{4,5},{5,4},{6,7},{7,6},{8,9},{9,8},{10,11... | collective-permute-start | bytes 196616 | tf_op jit(solution)/shard_map/ppermute | solution.py:274
  16.6 4.2 %collective-permute-start.7 = (bf16[2,136,128]{2,1,0:T(8,128)(2,1)S(1)}, bf16[2,136,128]{2,1,0:T(8,128)(2,1)S(1)}, u32[]{:S(2)}, u32[]{:S(2)}) collective-permute-start(bf16[2,136,128]{2,1,0:T(8,128)(2,1)S(1)} %get-tuple-element.30), channel_id=1, source_target_pairs={{0,1},{1,0},{2,3},{3,2},{4,5},{5,4},{6,7},{7,6},{8,9},{9,8},{10,11... | collective-permute-start | bytes 208904 | tf_op jit(solution)/shard_map/ppermute | solution.py:274
  18.8 4.3 %collective-permute-start.4 = (bf16[4,136,128]{2,1,0:T(8,128)(2,1)S(1)}, bf16[4,136,128]{2,1,0:T(8,128)(2,1)S(1)}, u32[]{:S(2)}, u32[]{:S(2)}) collective-permute-start(bf16[4,136,128]{2,1,0:T(8,128)(2,1)S(1)} %get-tuple-element.27), channel_id=1, source_target_pairs={{0,1},{1,0},{2,3},{3,2},{4,5},{5,4},{6,7},{7,6},{8,9},{9,8},{10,11... | collective-permute-start | bytes 417800 | tf_op jit(solution)/shard_map/ppermute | solution.py:274
  20.6 1.6 %collective-permute-start.11 = (bf16[2,136,128]{2,1,0:T(8,128)(2,1)S(1)}, bf16[2,136,128]{2,1,0:T(8,128)(2,1)S(1)}, u32[]{:S(2)}, u32[]{:S(2)}) collective-permute-start(bf16[2,136,128]{2,1,0:T(8,128)(2,1)S(1)} %get-tuple-element.32), channel_id=1, source_target_pairs={{0,1},{1,0},{2,3},{3,2},{4,5},{5,4},{6,7},{7,6},{8,9},{9,8},{10,11... | collective-permute-start | bytes 208904 | tf_op jit(solution)/shard_map/ppermute | solution.py:274
  20.8 3.2 %collective-permute-start.8 = (bf16[2,136,128]{2,1,0:T(8,128)(2,1)S(1)}, bf16[2,136,128]{2,1,0:T(8,128)(2,1)S(1)}, u32[]{:S(2)}, u32[]{:S(2)}) collective-permute-start(bf16[2,136,128]{2,1,0:T(8,128)(2,1)S(1)} %shard_map.59), channel_id=1, source_target_pairs={{0,2},{1,3},{2,0},{3,1},{4,6},{5,7},{6,4},{7,5},{8,10},{9,11},{10,... | collective-permute-start | bytes 208904 | tf_op jit(solution)/shard_map/ppermute | solution.py:274
  22.3 3.4 %collective-permute-start.12 = (bf16[2,136,128]{2,1,0:T(8,128)(2,1)S(1)}, bf16[2,136,128]{2,1,0:T(8,128)(2,1)S(1)}, u32[]{:S(2)}, u32[]{:S(2)}) collective-permute-start(bf16[2,136,128]{2,1,0:T(8,128)(2,1)S(1)} %shard_map.61), channel_id=1, source_target_pairs={{0,2},{1,3},{2,0},{3,1},{4,6},{5,7},{6,4},{7,5},{8,10},{9,11},{10,... | collective-permute-start | bytes 208904 | tf_op jit(solution)/shard_map/ppermute | solution.py:274
  25.9 5.3 %collective-permute-start.13 = (bf16[136,128]{1,0:T(8,128)(2,1)S(1)}, bf16[136,128]{1,0:T(8,128)(2,1)S(1)}, u32[]{:S(2)}, u32[]{:S(2)}) collective-permute-start(bf16[136,128]{1,0:T(8,128)(2,1)S(1)} %get-tuple-element.34), channel_id=1, source_target_pairs={{0,4},{1,5},{2,6},{3,7},{4,0},{5,1},{6,2},{7,3},{8,12},{9,13},{10,... | collective-permute-start | bytes 104456 | tf_op jit(solution)/shard_map/ppermute | solution.py:274
  27.3 4.3 %collective-permute-start.14 = (bf16[136,128]{1,0:T(8,128)(2,1)S(1)}, bf16[136,128]{1,0:T(8,128)(2,1)S(1)}, u32[]{:S(2)}, u32[]{:S(2)}) collective-permute-start(bf16[136,128]{1,0:T(8,128)(2,1)S(1)} %get-tuple-element.35), channel_id=1, source_target_pairs={{0,9},{1,8},{2,11},{3,10},{4,13},{5,12},{6,15},{7,14},{8,1},{9,0},... | collective-permute-start | bytes 104456 | tf_op jit(solution)/shard_map/ppermute | solution.py:274
  29.9 5.2 %collective-permute-start.15 = (bf16[136,128]{1,0:T(8,128)(2,1)S(1)}, bf16[136,128]{1,0:T(8,128)(2,1)S(1)}, u32[]{:S(2)}, u32[]{:S(2)}) collective-permute-start(bf16[136,128]{1,0:T(8,128)(2,1)S(1)} %get-tuple-element.36), channel_id=1, source_target_pairs={{0,13},{1,12},{2,15},{3,14},{4,9},{5,8},{6,11},{7,10},{8,5},{9,4},... | collective-permute-start | bytes 104456 | tf_op jit(solution)/shard_map/ppermute | solution.py:274

commit v5 on v4

--- a/solution.py
+++ b/solution.py
@@ -232,7 +232,7 @@
     got_refs, out_ref = refs[:-1], refs[-1]
     parts = [unkept(keep_ref[...])] + [unpacked(got[...]) for got in got_refs]
     num, _, total = merged(parts)
-    out_ref[...] = (num / total).T.astype(jnp.bfloat16)
+    out_ref[...] = (num / total).astype(jnp.bfloat16).T
 
 
 def call(kernel, outs, specs, flops=0, nbytes=0, grant=4, scratch=()):

time: 36 us -> 36 us (level)
  no operation moved by 1% of the time
where the time goes in v5:
time: 36 us; the launch traced here: 35.8 us
  starting transfers between devices  17.1 us (48%)
  waiting for transfers between devices  11.1 us (31%)
  Pallas kernels  7.51 us (21%)
    ppermute x16, starting transfers between devices, swap(): return lax.ppermute(part, 'blk', pairs(shards, mask))  17.1 us
    ppermute x16, waiting for transfers between devices, swap(): return lax.ppermute(part, 'blk', pairs(shards, mask))  11.1 us
    pallas_call x3, Pallas kernels, attend(): call(functools.partial(attend_kernel, [False, True], cut[0]), [struct((he...  4.64 us
    pallas_call x1, Pallas kernels, program(): call(functools.partial(prep_kernel, local_rows, (near_origin, far_origin)...  1.78 us
  transfers between devices with their start and end apart: 16, of which 8 were waited for; matrix products, arithmetic and copies ran while one was open for 0% of the time, Pallas kernels for 18%

profile of v5, /device:TPU:1, one launch (start us, length us, event | category | flops | bytes accessed | tf_op | source)
XLA Modules:
  0.0 35.8 jit_solution(1249437357319836376)
XLA Ops:
  0.0 4.7 %collective-permute-start.2 = (bf16[4,32,128]{2,1,0:T(8,128)(2,1)}, bf16[4,32,128]{2,1,0:T(8,128)(2,1)S(1)}, u32[]{:S(2)}, u32[]{:S(2)}) collective-permute-start(bf16[4,32,128]{2,1,0:T(8,128)(2,1)} %bitcast.11), channel_id=1, source_target_pairs={{0,13},{1,12},{2,15},{3,14},{4,9},{5,8},{6,11},{7,10},{8,5},{9,4},... | collective-permute-start | bytes 98312 | tf_op jit(solution)/shard_map/ppermute | solution.py:274
  4.7 0.0 collective-permute-start.1
  4.7 0.3 collective-permute-start
  5.0 1.8 %shard_map.55 = (bf16[4,32,128]{2,1,0:T(8,128)(2,1)S(1)}, bf16[2,1280,256]{2,1,0:T(8,128)(2,1)S(1)}, bf16[4,136,1280]{2,1,0:T(8,128)(2,1)S(1)}, bf16[2,1280,128]...) custom-call(s32[1]{0:T(128)} %bitcast.info_ref, s32[2]{0:T(128)} %len_hbm.1, ...), custom_call_target="tpu_custom_call" | custom-call | bytes 2621440 | tf_op jit(solution)/shard_map/pallas_call | solution.py:283
  6.8 1.2 %collective-permute-done = bf16[4,32,128]{2,1,0:T(8,128)(2,1)S(1)} collective-permute-done((bf16[4,32,128]{2,1,0:T(8,128)(2,1)}, bf16[4,32,128]{2,1,0:T(8,128)(2,1)S(1)}, u32[]{:S(2)}, u32[]{:S(2)}) %collective-permute-start) | collective-permute-done | bytes 32800 | tf_op jit(solution)/shard_map/ppermute | solution.py:274
  8.0 1.1 %collective-permute-done.1 = bf16[4,32,128]{2,1,0:T(8,128)(2,1)S(1)} collective-permute-done((bf16[4,32,128]{2,1,0:T(8,128)(2,1)}, bf16[4,32,128]{2,1,0:T(8,128)(2,1)S(1)}, u32[]{:S(2)}, u32[]{:S(2)}) %collective-permute-start.1) | collective-permute-done | bytes 32800 | tf_op jit(solution)/shard_map/ppermute | solution.py:274
  9.2 0.0 collective-permute-done.2
  9.2 1.3 %collective-permute-start.5 = (bf16[2,128,128]{2,1,0:T(8,128)(2,1)S(1)}, bf16[2,128,128]{2,1,0:T(8,128)(2,1)S(1)}, u32[]{:S(2)}, u32[]{:S(2)}) collective-permute-start(bf16[2,128,128]{2,1,0:T(8,128)(2,1)S(1)} %get-tuple-element.37), channel_id=1, source_target_pairs={{0,2},{1,3},{2,0},{3,1},{4,6},{5,7},{6,4},{7,5},{8,10},{9,11},{10,... | collective-permute-start | bytes 196616 | tf_op jit(solution)/shard_map/ppermute | solution.py:274
  10.5 0.3 collective-permute-start.3
  10.8 0.2 collective-permute-start.9
  11.0 1.8 %collective-permute-done.5.refs_0_ = bf16[2,128,128]{2,1,0:T(8,128)(2,1)S(1)} collective-permute-done((bf16[2,128,128]{2,1,0:T(8,128)(2,1)S(1)}, bf16[2,128,128]{2,1,0:T(8,128)(2,1)S(1)}, u32[]{:S(2)}, u32[]{:S(2)}) %collective-permute-start.5) | collective-permute-done | bytes 65568 | tf_op jit(solution)/shard_map/ppermute | solution.py:274
  12.9 0.9 %collective-permute-start.6 = (bf16[2,128,128]{2,1,0:T(8,128)(2,1)S(1)}, bf16[2,128,128]{2,1,0:T(8,128)(2,1)S(1)}, u32[]{:S(2)}, u32[]{:S(2)}) collective-permute-start(bf16[2,128,128]{2,1,0:T(8,128)(2,1)S(1)} %collective-permute-done.5.refs_0_), channel_id=1, source_target_pairs={{0,1},{1,0},{2,3},{3,2},{4,5},{5,4},{6,7},{7,6},{8,9},{9,8},{10,11... | collective-permute-start | bytes 196616 | tf_op jit(solution)/shard_map/ppermute | solution.py:274
  13.8 0.5 %collective-permute-done.9.refs_0_ = bf16[2,128,128]{2,1,0:T(8,128)(2,1)S(1)} collective-permute-done((bf16[2,128,128]{2,1,0:T(8,128)(2,1)S(1)}, bf16[2,128,128]{2,1,0:T(8,128)(2,1)S(1)}, u32[]{:S(2)}, u32[]{:S(2)}) %collective-permute-start.9) | collective-permute-done | bytes 65568 | tf_op jit(solution)/shard_map/ppermute | solution.py:274
  14.3 1.1 %collective-permute-start.10 = (bf16[2,128,128]{2,1,0:T(8,128)(2,1)S(1)}, bf16[2,128,128]{2,1,0:T(8,128)(2,1)S(1)}, u32[]{:S(2)}, u32[]{:S(2)}) collective-permute-start(bf16[2,128,128]{2,1,0:T(8,128)(2,1)S(1)} %collective-permute-done.9.refs_0_), channel_id=1, source_target_pairs={{0,1},{1,0},{2,3},{3,2},{4,5},{5,4},{6,7},{7,6},{8,9},{9,8},{10,11... | collective-permute-start | bytes 196616 | tf_op jit(solution)/shard_map/ppermute | solution.py:274
  15.3 0.0 collective-permute-done.6.refs_1_
  15.3 1.2 %shard_map.58 = (f32[2,136,128]{2,1,0:T(8,128)S(1)}, bf16[2,136,128]{2,1,0:T(8,128)(2,1)S(1)}) custom-call(s32[1]{0:T(128)} %bitcast.info_ref, bf16[2,128,128]{2,1,0:T(8,128)(2,1)S(1)} %collective-permute-done.5.refs_0_, bf16[2,128,128]{2,1,0:T(8,128)(2,1)S(1)} %collective-permute-done.6.refs_1_, bf16[2,1280,256]{2,1,0:T(8,128)(2,1)S(1)} %get-tuple-element.22.refs_2_, ...), custom_call_target="tpu_custom_call" | custom-call | flops 503316480 | tf_op jit(solution)/shard_map/pallas_call | solution.py:312
  16.6 0.1 collective-permute-start.7
  16.6 0.0 collective-permute-done.3.refs_1_
  16.6 2.2 %shard_map.56 = (f32[4,136,128]{2,1,0:T(8,128)S(1)}, bf16[4,136,128]{2,1,0:T(8,128)(2,1)S(1)}) custom-call(s32[1]{0:T(128)} %bitcast.info_ref, bf16[4,128,128]{2,1,0:T(8,128)(2,1)S(1)} %constant_dynamic-update-slice_fusion.refs_0_, bf16[4,128,128]{2,1,0:T(8,128)(2,1)S(1)} %collective-permute-done.3.refs_1_, ...), custom_call_target="tpu_custom_call" | custom-call | flops 1006632960 | tf_op jit(solution)/shard_map/pallas_call | solution.py:312
  18.8 0.5 %collective-permute-start.4 = (bf16[4,136,128]{2,1,0:T(8,128)(2,1)S(1)}, bf16[4,136,128]{2,1,0:T(8,128)(2,1)S(1)}, u32[]{:S(2)}, u32[]{:S(2)}) collective-permute-start(bf16[4,136,128]{2,1,0:T(8,128)(2,1)S(1)} %get-tuple-element.27), channel_id=1, source_target_pairs={{0,1},{1,0},{2,3},{3,2},{4,5},{5,4},{6,7},{7,6},{8,9},{9,8},{10,11... | collective-permute-start | bytes 417800 | tf_op jit(solution)/shard_map/ppermute | solution.py:274
  19.4 0.0 collective-permute-done.10.refs_1_
  19.4 1.2 %shard_map.60 = (f32[2,136,128]{2,1,0:T(8,128)S(1)}, bf16[2,136,128]{2,1,0:T(8,128)(2,1)S(1)}) custom-call(s32[1]{0:T(128)} %bitcast.info_ref, bf16[2,128,128]{2,1,0:T(8,128)(2,1)S(1)} %collective-permute-done.9.refs_0_, bf16[2,128,128]{2,1,0:T(8,128)(2,1)S(1)} %collective-permute-done.10.refs_1_, bf16[2,1280,256]{2,1,0:T(8,128)(2,1)S(1)} %get-tuple-element.22.refs_2_, ...), custom_call_target="tpu_custom_call" | custom-call | flops 503316480 | tf_op jit(solution)/shard_map/pallas_call | solution.py:312
  20.6 0.1 collective-permute-start.11
  20.7 0.0 collective-permute-done.7.got_ref
  20.8 1.4 %collective-permute-start.8 = (bf16[2,136,128]{2,1,0:T(8,128)(2,1)S(1)}, bf16[2,136,128]{2,1,0:T(8,128)(2,1)S(1)}, u32[]{:S(2)}, u32[]{:S(2)}) collective-permute-start(bf16[2,136,128]{2,1,0:T(8,128)(2,1)S(1)} %shard_map.59), channel_id=1, source_target_pairs={{0,2},{1,3},{2,0},{3,1},{4,6},{5,7},{6,4},{7,5},{8,10},{9,11},{10,... | collective-permute-start | bytes 208904 | tf_op jit(solution)/shard_map/ppermute | solution.py:274
  22.2 0.0 collective-permute-done.11.got_ref
  22.3 0.9 %collective-permute-start.12 = (bf16[2,136,128]{2,1,0:T(8,128)(2,1)S(1)}, bf16[2,136,128]{2,1,0:T(8,128)(2,1)S(1)}, u32[]{:S(2)}, u32[]{:S(2)}) collective-permute-start(bf16[2,136,128]{2,1,0:T(8,128)(2,1)S(1)} %shard_map.61), channel_id=1, source_target_pairs={{0,2},{1,3},{2,0},{3,1},{4,6},{5,7},{6,4},{7,5},{8,10},{9,11},{10,... | collective-permute-start | bytes 208904 | tf_op jit(solution)/shard_map/ppermute | solution.py:274
  23.1 0.0 collective-permute-done.4.got_ref
  23.1 0.1 shard_map.57.keep_ref
  23.2 0.8 %collective-permute-done.8 = bf16[2,136,128]{2,1,0:T(8,128)(2,1)S(1)} collective-permute-done((bf16[2,136,128]{2,1,0:T(8,128)(2,1)S(1)}, bf16[2,136,128]{2,1,0:T(8,128)(2,1)S(1)}, u32[]{:S(2)}, u32[]{:S(2)}) %collective-permute-start.8) | collective-permute-done | bytes 69664 | tf_op jit(solution)/shard_map/ppermute | solution.py:274
  24.0 1.7 %collective-permute-done.12 = bf16[2,136,128]{2,1,0:T(8,128)(2,1)S(1)} collective-permute-done((bf16[2,136,128]{2,1,0:T(8,128)(2,1)S(1)}, bf16[2,136,128]{2,1,0:T(8,128)(2,1)S(1)}, u32[]{:S(2)}, u32[]{:S(2)}) %collective-permute-start.12) | collective-permute-done | bytes 69664 | tf_op jit(solution)/shard_map/ppermute | solution.py:274
  25.7 0.2 shard_map.62
  25.9 1.4 %collective-permute-start.13 = (bf16[136,128]{1,0:T(8,128)(2,1)S(1)}, bf16[136,128]{1,0:T(8,128)(2,1)S(1)}, u32[]{:S(2)}, u32[]{:S(2)}) collective-permute-start(bf16[136,128]{1,0:T(8,128)(2,1)S(1)} %get-tuple-element.34), channel_id=1, source_target_pairs={{0,4},{1,5},{2,6},{3,7},{4,0},{5,1},{6,2},{7,3},{8,12},{9,13},{10,... | collective-permute-start | bytes 104456 | tf_op jit(solution)/shard_map/ppermute | solution.py:274
  27.3 2.6 %collective-permute-start.14 = (bf16[136,128]{1,0:T(8,128)(2,1)S(1)}, bf16[136,128]{1,0:T(8,128)(2,1)S(1)}, u32[]{:S(2)}, u32[]{:S(2)}) collective-permute-start(bf16[136,128]{1,0:T(8,128)(2,1)S(1)} %get-tuple-element.35), channel_id=1, source_target_pairs={{0,9},{1,8},{2,11},{3,10},{4,13},{5,12},{6,15},{7,14},{8,1},{9,0},... | collective-permute-start | bytes 104456 | tf_op jit(solution)/shard_map/ppermute | solution.py:274
  29.9 1.3 %collective-permute-start.15 = (bf16[136,128]{1,0:T(8,128)(2,1)S(1)}, bf16[136,128]{1,0:T(8,128)(2,1)S(1)}, u32[]{:S(2)}, u32[]{:S(2)}) collective-permute-start(bf16[136,128]{1,0:T(8,128)(2,1)S(1)} %get-tuple-element.36), channel_id=1, source_target_pairs={{0,13},{1,12},{2,15},{3,14},{4,9},{5,8},{6,11},{7,10},{8,5},{9,4},... | collective-permute-start | bytes 104456 | tf_op jit(solution)/shard_map/ppermute | solution.py:274
  31.2 0.0 collective-permute-done.13.refs_0_
  31.2 0.4 %collective-permute-done.14.refs_1_ = bf16[136,128]{1,0:T(8,128)(2,1)S(1)} collective-permute-done((bf16[136,128]{1,0:T(8,128)(2,1)S(1)}, bf16[136,128]{1,0:T(8,128)(2,1)S(1)}, u32[]{:S(2)}, u32[]{:S(2)}) %collective-permute-start.14) | collective-permute-done | bytes 34848 | tf_op jit(solution)/shard_map/ppermute | solution.py:274
  31.6 3.5 %collective-permute-done.15.refs_2_ = bf16[136,128]{1,0:T(8,128)(2,1)S(1)} collective-permute-done((bf16[136,128]{1,0:T(8,128)(2,1)S(1)}, bf16[136,128]{1,0:T(8,128)(2,1)S(1)}, u32[]{:S(2)}, u32[]{:S(2)}) %collective-permute-start.15) | collective-permute-done | bytes 34848 | tf_op jit(solution)/shard_map/ppermute | solution.py:274
  35.1 0.7 %shard_map.63 = bf16[128,128]{1,0:T(8,128)(2,1)} custom-call(f32[136,128]{1,0:T(8,128)S(1)} %get-tuple-element.33.keep_ref, bf16[136,128]{1,0:T(8,128)(2,1)S(1)} %collective-permute-done.13.refs_0_, bf16[136,128]{1,0:T(8,128)(2,1)S(1)} %collective-permute-done.14.refs_1_, bf16[136,128]{1,0:T(8,128)(2,1)S(1)} %collective-permute-done.15.refs_2_), custom_call_target="tpu_custom_call" | custom-call | tf_op jit(solution)/shard_map/pallas_call | solution.py:358
  (8 shorter events, 0.2 us)
Async XLA Ops:
  0.0 9.2 %collective-permute-start.2 = (bf16[4,32,128]{2,1,0:T(8,128)(2,1)}, bf16[4,32,128]{2,1,0:T(8,128)(2,1)S(1)}, u32[]{:S(2)}, u32[]{:S(2)}) collective-permute-start(bf16[4,32,128]{2,1,0:T(8,128)(2,1)} %bitcast.11), channel_id=1, source_target_pairs={{0,13},{1,12},{2,15},{3,14},{4,9},{5,8},{6,11},{7,10},{8,5},{9,4},... | collective-permute-start | bytes 98312 | tf_op jit(solution)/shard_map/ppermute | solution.py:274
  4.7 4.4 %collective-permute-start.1 = (bf16[4,32,128]{2,1,0:T(8,128)(2,1)}, bf16[4,32,128]{2,1,0:T(8,128)(2,1)S(1)}, u32[]{:S(2)}, u32[]{:S(2)}) collective-permute-start(bf16[4,32,128]{2,1,0:T(8,128)(2,1)} %bitcast.12), channel_id=1, source_target_pairs={{0,9},{1,8},{2,11},{3,10},{4,13},{5,12},{6,15},{7,14},{8,1},{9,0},... | collective-permute-start | bytes 98312 | tf_op jit(solution)/shard_map/ppermute | solution.py:274
  4.7 3.3 %collective-permute-start = (bf16[4,32,128]{2,1,0:T(8,128)(2,1)}, bf16[4,32,128]{2,1,0:T(8,128)(2,1)S(1)}, u32[]{:S(2)}, u32[]{:S(2)}) collective-permute-start(bf16[4,32,128]{2,1,0:T(8,128)(2,1)} %bitcast.13), channel_id=1, source_target_pairs={{0,4},{1,5},{2,6},{3,7},{4,0},{5,1},{6,2},{7,3},{8,12},{9,13},{10,... | collective-permute-start | bytes 98312 | tf_op jit(solution)/shard_map/ppermute | solution.py:274
  9.2 3.7 %collective-permute-start.5 = (bf16[2,128,128]{2,1,0:T(8,128)(2,1)S(1)}, bf16[2,128,128]{2,1,0:T(8,128)(2,1)S(1)}, u32[]{:S(2)}, u32[]{:S(2)}) collective-permute-start(bf16[2,128,128]{2,1,0:T(8,128)(2,1)S(1)} %get-tuple-element.37), channel_id=1, source_target_pairs={{0,2},{1,3},{2,0},{3,1},{4,6},{5,7},{6,4},{7,5},{8,10},{9,11},{10,... | collective-permute-start | bytes 196616 | tf_op jit(solution)/shard_map/ppermute | solution.py:274
  10.5 6.1 %collective-permute-start.3 = (bf16[4,128,128]{2,1,0:T(8,128)(2,1)S(1)}, bf16[4,128,128]{2,1,0:T(8,128)(2,1)S(1)}, u32[]{:S(2)}, u32[]{:S(2)}) collective-permute-start(bf16[4,128,128]{2,1,0:T(8,128)(2,1)S(1)} %constant_dynamic-update-slice_fusion.refs_0_), channel_id=1, source_target_pairs={{0,1},{1,0},{2,3},{3,2},{4,5},{5,4},{6,7},{7,6},{8,9},{9,8},{10,11... | collective-permute-start | bytes 393224 | tf_op jit(solution)/shard_map/ppermute | solution.py:274
  10.8 3.4 %collective-permute-start.9 = (bf16[2,128,128]{2,1,0:T(8,128)(2,1)S(1)}, bf16[2,128,128]{2,1,0:T(8,128)(2,1)S(1)}, u32[]{:S(2)}, u32[]{:S(2)}) collective-permute-start(bf16[2,128,128]{2,1,0:T(8,128)(2,1)S(1)} %get-tuple-element.38), channel_id=1, source_target_pairs={{0,2},{1,3},{2,0},{3,1},{4,6},{5,7},{6,4},{7,5},{8,10},{9,11},{10,... | collective-permute-start | bytes 196616 | tf_op jit(solution)/shard_map/ppermute | solution.py:274
  12.9 2.4 %collective-permute-start.6 = (bf16[2,128,128]{2,1,0:T(8,128)(2,1)S(1)}, bf16[2,128,128]{2,1,0:T(8,128)(2,1)S(1)}, u32[]{:S(2)}, u32[]{:S(2)}) collective-permute-start(bf16[2,128,128]{2,1,0:T(8,128)(2,1)S(1)} %collective-permute-done.5.refs_0_), channel_id=1, source_target_pairs={{0,1},{1,0},{2,3},{3,2},{4,5},{5,4},{6,7},{7,6},{8,9},{9,8},{10,11... | collective-permute-start | bytes 196616 | tf_op jit(solution)/shard_map/ppermute | solution.py:274
  14.3 5.1 %collective-permute-start.10 = (bf16[2,128,128]{2,1,0:T(8,128)(2,1)S(1)}, bf16[2,128,128]{2,1,0:T(8,128)(2,1)S(1)}, u32[]{:S(2)}, u32[]{:S(2)}) collective-permute-start(bf16[2,128,128]{2,1,0:T(8,128)(2,1)S(1)} %collective-permute-done.9.refs_0_), channel_id=1, source_target_pairs={{0,1},{1,0},{2,3},{3,2},{4,5},{5,4},{6,7},{7,6},{8,9},{9,8},{10,11... | collective-permute-start | bytes 196616 | tf_op jit(solution)/shard_map/ppermute | solution.py:274
  16.6 4.2 %collective-permute-start.7 = (bf16[2,136,128]{2,1,0:T(8,128)(2,1)S(1)}, bf16[2,136,128]{2,1,0:T(8,128)(2,1)S(1)}, u32[]{:S(2)}, u32[]{:S(2)}) collective-permute-start(bf16[2,136,128]{2,1,0:T(8,128)(2,1)S(1)} %get-tuple-element.30), channel_id=1, source_target_pairs={{0,1},{1,0},{2,3},{3,2},{4,5},{5,4},{6,7},{7,6},{8,9},{9,8},{10,11... | collective-permute-start | bytes 208904 | tf_op jit(solution)/shard_map/ppermute | solution.py:274
  18.8 4.3 %collective-permute-start.4 = (bf16[4,136,128]{2,1,0:T(8,128)(2,1)S(1)}, bf16[4,136,128]{2,1,0:T(8,128)(2,1)S(1)}, u32[]{:S(2)}, u32[]{:S(2)}) collective-permute-start(bf16[4,136,128]{2,1,0:T(8,128)(2,1)S(1)} %get-tuple-element.27), channel_id=1, source_target_pairs={{0,1},{1,0},{2,3},{3,2},{4,5},{5,4},{6,7},{7,6},{8,9},{9,8},{10,11... | collective-permute-start | bytes 417800 | tf_op jit(solution)/shard_map/ppermute | solution.py:274
  20.6 1.6 %collective-permute-start.11 = (bf16[2,136,128]{2,1,0:T(8,128)(2,1)S(1)}, bf16[2,136,128]{2,1,0:T(8,128)(2,1)S(1)}, u32[]{:S(2)}, u32[]{:S(2)}) collective-permute-start(bf16[2,136,128]{2,1,0:T(8,128)(2,1)S(1)} %get-tuple-element.32), channel_id=1, source_target_pairs={{0,1},{1,0},{2,3},{3,2},{4,5},{5,4},{6,7},{7,6},{8,9},{9,8},{10,11... | collective-permute-start | bytes 208904 | tf_op jit(solution)/shard_map/ppermute | solution.py:274
  20.8 3.2 %collective-permute-start.8 = (bf16[2,136,128]{2,1,0:T(8,128)(2,1)S(1)}, bf16[2,136,128]{2,1,0:T(8,128)(2,1)S(1)}, u32[]{:S(2)}, u32[]{:S(2)}) collective-permute-start(bf16[2,136,128]{2,1,0:T(8,128)(2,1)S(1)} %shard_map.59), channel_id=1, source_target_pairs={{0,2},{1,3},{2,0},{3,1},{4,6},{5,7},{6,4},{7,5},{8,10},{9,11},{10,... | collective-permute-start | bytes 208904 | tf_op jit(solution)/shard_map/ppermute | solution.py:274
  22.3 3.4 %collective-permute-start.12 = (bf16[2,136,128]{2,1,0:T(8,128)(2,1)S(1)}, bf16[2,136,128]{2,1,0:T(8,128)(2,1)S(1)}, u32[]{:S(2)}, u32[]{:S(2)}) collective-permute-start(bf16[2,136,128]{2,1,0:T(8,128)(2,1)S(1)} %shard_map.61), channel_id=1, source_target_pairs={{0,2},{1,3},{2,0},{3,1},{4,6},{5,7},{6,4},{7,5},{8,10},{9,11},{10,... | collective-permute-start | bytes 208904 | tf_op jit(solution)/shard_map/ppermute | solution.py:274
  25.9 5.3 %collective-permute-start.13 = (bf16[136,128]{1,0:T(8,128)(2,1)S(1)}, bf16[136,128]{1,0:T(8,128)(2,1)S(1)}, u32[]{:S(2)}, u32[]{:S(2)}) collective-permute-start(bf16[136,128]{1,0:T(8,128)(2,1)S(1)} %get-tuple-element.34), channel_id=1, source_target_pairs={{0,4},{1,5},{2,6},{3,7},{4,0},{5,1},{6,2},{7,3},{8,12},{9,13},{10,... | collective-permute-start | bytes 104456 | tf_op jit(solution)/shard_map/ppermute | solution.py:274
  27.3 4.3 %collective-permute-start.14 = (bf16[136,128]{1,0:T(8,128)(2,1)S(1)}, bf16[136,128]{1,0:T(8,128)(2,1)S(1)}, u32[]{:S(2)}, u32[]{:S(2)}) collective-permute-start(bf16[136,128]{1,0:T(8,128)(2,1)S(1)} %get-tuple-element.35), channel_id=1, source_target_pairs={{0,9},{1,8},{2,11},{3,10},{4,13},{5,12},{6,15},{7,14},{8,1},{9,0},... | collective-permute-start | bytes 104456 | tf_op jit(solution)/shard_map/ppermute | solution.py:274
  29.9 5.2 %collective-permute-start.15 = (bf16[136,128]{1,0:T(8,128)(2,1)S(1)}, bf16[136,128]{1,0:T(8,128)(2,1)S(1)}, u32[]{:S(2)}, u32[]{:S(2)}) collective-permute-start(bf16[136,128]{1,0:T(8,128)(2,1)S(1)} %get-tuple-element.36), channel_id=1, source_target_pairs={{0,13},{1,12},{2,15},{3,14},{4,9},{5,8},{6,11},{7,10},{8,5},{9,4},... | collective-permute-start | bytes 104456 | tf_op jit(solution)/shard_map/ppermute | solution.py:274
